TPU v7x, 128 devices: a whole 4x4x4 slice. The times are simulated.
128 devices in a mesh: replica: 16 (over z_hi, x, core), shard: 8 (over z_lo, y).
Axes of the slice: x: 4, y: 4, z: 4 (z_hi: 2, z_lo: 2; z = z_hi * 2 + z_lo), core: 2. Of those that a mesh axis runs over, the one named last changes fastest.
Arguments:
- features: bfloat16 [32768, 8192], P(('replica', 'shard')), may hold values from -24 to 24
- key_grads: bfloat16 [32768, 1024], P(('replica', 'shard')), may hold values from -1.5 to 1.5
- key_weight: bfloat16 [8192, 1024], P('shard'), may hold values from -0.1875 to 0.1875
- momentum: float32 [16, 8192, 1024], P('replica', 'shard'), may hold values from -8 to 8
- worker_error: float32 [16, 8192, 1024], P('replica', 'shard'), may hold values from -2 to 2
- server_error: float32 [8, 1024, 1024], P('shard', 'replica'), may hold values from -2 to 2
Outputs:
- input_grads: bfloat16 [32768, 8192], P(('replica', 'shard'))
- synced_momentum: bfloat16 [8192, 1024], P('shard')
- new_worker_error: float32 [16, 8192, 1024], P('replica', 'shard')
- new_server_error: float32 [8, 1024, 1024], P('shard', 'replica')
All inputs are finite; a program needn't handle non-finite values. Where the computation divides by a largest or mean magnitude, that divisor is 1e-20 or more.
Results may differ from a plain program's by a relative error of at most 0.018.
Values may be sent and summed in bfloat16 or wider, within the bound.
No kernel may reach another device: no remote copies, remote signals or barrier semaphores. Data moves between devices by JAX's collectives and lax.ppermute only.
A program may use at most 128 MiB of HBM per device.

v0:
```python
import jax
import jax.numpy as jnp
from jax import lax
from jax.experimental import pallas as pl
from jax.experimental.pallas import tpu as pltpu
from jax.sharding import Mesh
from jax.sharding import PartitionSpec as P


decay_rate = 0.9
TOK = 256
BLK = 1024
KV = 1024
OWN = 64
SHARD = ("zl", "y")
CHIPS = ("zh", "x")
Z = ("zh", "core", "zl")
SWAP = [(0, 1), (1, 0)]


def compress(values):
    scale = jnp.mean(jnp.abs(values), axis=-1, keepdims=True) + 1e-06
    return (scale * jnp.tanh(values / scale)).astype(jnp.bfloat16)


def shift_y(step):
    return [(i, (i + step) % 4) for i in range(4)]


def shard_perm(dz, dy):
    return [(((z + dz) % 2) * 4 + (y + dy) % 4, z * 4 + y) for z in range(2) for y in range(4)]


def z_perm():
    pairs = []
    for zh in range(2):
        for zl in range(2):
            z = zh * 2 + zl
            other = (z + 1) % 4 if z % 2 == 1 else (z + 3) % 4
            pairs.append(((zh * 2 + 0) * 2 + zl, (zh * 2 + 0) * 2 + (1 - zl)))
            pairs.append(((zh * 2 + 1) * 2 + zl, ((other // 2) * 2 + 1) * 2 + other % 2))
    return pairs


def contract_tokens(feats, keys):
    acc = None
    for f, k in zip(feats, keys):
        part = lax.dot_general(
            f[...], k[...], (((0,), (0,)), ((), ())), preferred_element_type=jnp.float32
        )
        acc = part if acc is None else acc + part
    return acc


def first_kernel(f, k, momentum, worker, out):
    acc = contract_tokens([f], [k])
    out[...] = decay_rate * momentum[...] + (1.0 - decay_rate) * acc + worker[...]


def early_kernel(n, *refs):
    base, out = refs[2 * n :]
    out[...] = base[...] + (1.0 - decay_rate) * contract_tokens(refs[:n], refs[n : 2 * n])


def early_call(kernel, feats, keys, rest, rows=256):
    n = len(feats)
    feat_spec = pl.BlockSpec((TOK, rows), lambda i: (0, i))
    key_spec = pl.BlockSpec((TOK, KV), lambda i: (0, 0))
    row_spec = pl.BlockSpec((rows, KV), lambda i: (i, 0))
    return pl.pallas_call(
        kernel,
        out_shape=jax.ShapeDtypeStruct((BLK, KV), jnp.float32),
        grid=(BLK // rows,),
        in_specs=[feat_spec] * n + [key_spec] * n + [row_spec] * len(rest),
        out_specs=row_spec,
        cost_estimate=pl.CostEstimate(
            flops=2 * n * TOK * BLK * KV,
            bytes_accessed=(4 + 4 * len(rest) + n) * 2**20,
            transcendentals=0,
        ),
    )(*feats, *keys, *rest)


def late_kernel(feat_rows, key_rows, core_ref, *refs):
    n, m = len(feat_rows), len(key_rows)
    base, new_worker, mine, other = refs[n + m :]
    feats, keys = [], []
    at = 0
    for ref, size in zip(refs[n : n + m], key_rows):
        keys.append(ref)
        block, start = at // TOK, at % TOK
        feats.append(refs[block].at[pl.ds(start, size), :])
        at += size
    acc = contract_tokens(feats, keys)
    value = base[...] + (1.0 - decay_rate) * acc
    packed = compress(value)
    new_worker[...] = value - packed.astype(jnp.float32)
    groups = packed.reshape(-1, 2, OWN, KV)
    first = core_ref[0] == 0
    mine[...] = jnp.where(first, groups[:, 0], groups[:, 1])
    other[...] = jnp.where(first, groups[:, 1], groups[:, 0])


def late_call(core, feats, keys, base, rows=256):
    chunk = rows // (2 * OWN)
    feat_rows = [f.shape[0] for f in feats]
    key_rows = [k.shape[0] for k in keys]
    feat_spec = pl.BlockSpec((TOK, rows), lambda i, c: (0, i))
    key_specs = [pl.BlockSpec((r, KV), lambda i, c: (0, 0)) for r in key_rows]
    row_spec = pl.BlockSpec((rows, KV), lambda i, c: (i, 0))
    half_spec = pl.BlockSpec((chunk, OWN, KV), lambda i, c: (i, 0, 0))
    half = jax.ShapeDtypeStruct((BLK // (2 * OWN), OWN, KV), jnp.bfloat16)
    return pl.pallas_call(
        lambda *refs: late_kernel(feat_rows, key_rows, *refs),
        out_shape=(jax.ShapeDtypeStruct((BLK, KV), jnp.float32), half, half),
        grid_spec=pltpu.PrefetchScalarGridSpec(
            num_scalar_prefetch=1,
            grid=(BLK // rows,),
            in_specs=[feat_spec] * len(feats) + key_specs + [row_spec],
            out_specs=(row_spec, half_spec, half_spec),
        ),
        cost_estimate=pl.CostEstimate(
            flops=2 * sum(key_rows) * BLK * KV, bytes_accessed=14 * 2**20, transcendentals=BLK * KV
        ),
        name="late",
    )(core, *feats, *keys, base)


def back_kernel(core_ref, own, left, right, far_a, far_b, weight, got, got_other, *outs):
    j = pl.program_id(0)
    pair = jnp.where(core_ref[0] == j, got[...], got_other[...])

    def product(block, w):
        return lax.dot_general(
            block, w, (((1,), (1,)), ((), ())), preferred_element_type=jnp.float32
        ).astype(jnp.bfloat16)

    for dz, w in ((0, weight[...]), (1, pair)):
        for block, out in zip((own, left, right), outs[:3]):
            out[dz] = product(block[...], w)
        outs[3][dz, : TOK // 2] = product(far_a[...], w)
        outs[3][dz, TOK // 2 :] = product(far_b[...], w)


def back_call(core, blocks, weight, got, got_other):
    cols = BLK // 2

    def full(a):
        return pl.BlockSpec(a.shape, lambda j, c: (0, 0))

    out_spec = pl.BlockSpec((2, TOK, cols), lambda j, c: (0, 0, j))
    out = jax.ShapeDtypeStruct((2, TOK, BLK), jnp.bfloat16)
    return pl.pallas_call(
        back_kernel,
        out_shape=(out,) * 4,
        grid_spec=pltpu.PrefetchScalarGridSpec(
            num_scalar_prefetch=1,
            grid=(2,),
            in_specs=[full(b) for b in blocks]
            + [pl.BlockSpec((cols, KV), lambda j, c: (j, 0)), full(got), full(got_other)],
            out_specs=(out_spec,) * 4,
        ),
        cost_estimate=pl.CostEstimate(
            flops=2 * 4 * TOK * 2 * BLK * KV, bytes_accessed=10 * 2**20, transcendentals=0
        ),
        name="back",
    )(core, *blocks, weight, got, got_other)


def place_kernel(at_ref, *refs):
    pieces, out, buf, sem_in, sem_out = refs[:4], refs[4], refs[5], refs[6], refs[7]
    loads = [pltpu.make_async_copy(p, buf.at[i], sem_in.at[i]) for i, p in enumerate(pieces)]
    for load in loads:
        load.start()
    stores = []
    for i, load in enumerate(loads):
        load.wait()
        for dz in range(2):
            col = pl.multiple_of(at_ref[i, dz] * BLK, BLK)
            store = pltpu.make_async_copy(
                buf.at[i, dz], out.at[:, pl.ds(col, BLK)], sem_out.at[i, dz]
            )
            store.start()
            stores.append(store)
    for store in stores:
        store.wait()


def place_call(at, pieces):
    n = len(pieces)
    return pl.pallas_call(
        place_kernel,
        out_shape=jax.ShapeDtypeStruct((TOK, 8 * BLK), jnp.bfloat16),
        in_specs=[pl.BlockSpec(memory_space=pltpu.SMEM)] + [pl.BlockSpec(memory_space=pl.ANY)] * n,
        out_specs=pl.BlockSpec(memory_space=pl.ANY),
        scratch_shapes=[
            pltpu.VMEM((n, 2, TOK, BLK), jnp.bfloat16),
            pltpu.SemaphoreType.DMA((n,)),
            pltpu.SemaphoreType.DMA((n, 2)),
        ],
        cost_estimate=pl.CostEstimate(flops=0, bytes_accessed=8 * 2**20, transcendentals=0),
        name="place",
    )(at, *pieces)


def per_device(features, key_grads, key_weight, momentum, worker_error, server_error):
    zl, y = lax.axis_index("zl"), lax.axis_index("y")
    core = lax.axis_index("core")
    core_arg = core.reshape(1).astype(jnp.int32)
    fence = lax.optimization_barrier

    def columns(dz, dy):
        to = ((zl + dz) % 2) * 4 + (y + 4 - dy) % 4
        return lax.dynamic_slice_in_dim(features, to * BLK, BLK, axis=1)

    k10 = lax.ppermute(key_grads, "zl", SWAP)
    k03 = lax.ppermute(key_grads, "y", shift_y(1))
    k01 = lax.ppermute(key_grads, "y", shift_y(-1))
    half_weight = lax.dynamic_slice_in_dim(key_weight, core * (BLK // 2), BLK // 2, axis=0)
    order = [(0, 0), (1, 0), (0, 1), (0, 3), (1, 2), (1, 1), (1, 3), (0, 2)]
    pieces = {k: columns(*k) for k in order}
    flat = fence((k10, k03, k01, half_weight) + tuple(pieces.values()))
    k10, k03, k01, half_weight = flat[:4]
    pieces = dict(zip(order, flat[4:]))

    def send(key):
        return lax.ppermute(pieces[key], SHARD, shard_perm(*key))

    feats = {(0, 0): pieces[0, 0]}
    far_a = lax.ppermute(k03[: TOK // 2], "y", shift_y(1))
    far_b = lax.ppermute(k01[TOK // 2 :], "y", shift_y(-1))
    k13 = lax.ppermute(k10, "y", shift_y(1))
    k11 = lax.ppermute(k10, "y", shift_y(-1))
    got = lax.ppermute(half_weight, Z, z_perm())
    for key in order[1:5]:
        feats[key] = send(key)

    base = early_call(first_kernel, [feats[0, 0]], [key_grads], [momentum[0], worker_error[0]])

    flat = fence((far_a, far_b, k13, k11, got) + tuple(pieces[k] for k in order[5:]))
    far_a, far_b, k13, k11, got = flat[:5]
    pieces.update(zip(order[5:], flat[5:]))
    zfar_a = lax.ppermute(far_a, "zl", SWAP)
    zfar_b = lax.ppermute(far_b, "zl", SWAP)
    for key in order[5:]:
        feats[key] = send(key)

    got_other = lax.ppermute(got, "core", SWAP)
    early = [(1, 0), (0, 1), (0, 3)]
    early_keys = [k10, k01, k03]
    base = early_call(
        lambda *refs: early_kernel(len(early), *refs), [feats[k] for k in early], early_keys, [base]
    )
    backs = back_call(core_arg, (key_grads, k01, k03, far_a, far_b), key_weight, got, got_other)

    late = [(1, 1), (1, 3), (0, 2), (1, 2)]
    flat = fence(tuple(feats[k] for k in late) + (zfar_a, zfar_b, base) + tuple(backs))
    late_feats, (zfar_a, zfar_b, base), backs = flat[:4], flat[4:7], flat[7:]
    back_own, back_1, back_3, back_2 = backs
    home_1 = lax.ppermute(back_1, "y", shift_y(1))
    home_3 = lax.ppermute(back_3, "y", shift_y(-1))
    home_2 = lax.ppermute(back_2, "y", shift_y(2))
    new_worker, mine, other = late_call(
        core_arg, list(late_feats), [k11, k13, far_a, far_b, zfar_a, zfar_b], base
    )

    met = lax.ppermute(other, "core", SWAP)
    pair = (mine.astype(jnp.float32) + met.astype(jnp.float32)).astype(jnp.bfloat16)
    parts = lax.all_to_all(pair, CHIPS, 0, 0)
    held = jnp.sum(parts.astype(jnp.float32), axis=0) / 16 + server_error[0]
    block = compress(held)
    new_server = (held - block.astype(jnp.float32))[None]

    half = lax.all_to_all(jnp.broadcast_to(block[None], (8, OWN, KV)), CHIPS, 0, 0)
    half_other = lax.ppermute(half, "core", SWAP)
    is_mine = lax.broadcasted_iota(jnp.int32, (8, 2, OWN, KV), 1) == core
    synced = jnp.where(is_mine, half[:, None], half_other[:, None]).reshape(BLK, KV)

    dys = [0, 1, 3, 2]
    at = jnp.stack(
        [jnp.stack([((zl + dz) % 2) * 4 + (y + 4 - dy) % 4 for dz in range(2)]) for dy in dys]
    ).astype(jnp.int32)
    input_grads = place_call(at, [back_own, home_1, home_3, home_2])
    return input_grads, synced, new_worker[None], new_server


def solution(mesh):
    fine = Mesh(mesh.devices.reshape(2, 4, 2, 2, 4), ("zh", "x", "core", "zl", "y"))
    rep, shd = ("zh", "x", "core"), ("zl", "y")
    in_specs = (
        P(rep + shd, None),
        P(rep + shd, None),
        P(shd, None),
        P(rep, shd, None),
        P(rep, shd, None),
        P(shd, rep, None),
    )
    out_specs = (
        P(rep + shd, None),
        P(shd, None),
        P(rep, shd, None),
        P(shd, rep, None),
    )


    return jax.shard_map(
        per_device, mesh=fine, in_specs=in_specs, out_specs=out_specs, check_vma=False
    )
```

profile of v0, /device:TPU:1, one launch (start us, length us, event | category | flops | bytes accessed | tf_op | source)
XLA Modules:
  0.0 200.8 jit_solution(15641725414583942821)
XLA Ops:
  0.6 2.5 %collective-permute-start = (bf16[256,1024]{1,0:T(8,128)(2,1)}, bf16[256,1024]{1,0:T(8,128)(2,1)S(1)}, u32[]{:S(2)}, u32[]{:S(2)}) collective-permute-start(bf16[256,1024]{1,0:T(8,128)(2,1)} %own.1), channel_id=1, source_target_pairs={{0,4},{4,0},{1,5},{5,1},{2,6},{6,2},{3,7},{7,3},{8,12},{12,8},{9,1... | collective-permute-start | bytes 1572872 | tf_op jit(solution)/shard_map/ppermute | solution.py:216
  4.5 1.4 collective-permute-start.2
  7.2 4.2 %constant_dynamic-slice_fusion = (bf16[256,1024]{1,0:T(8,128)(2,1)}, bf16[256,1024]{1,0:T(8,128)(2,1)}, bf16[256,1024]{1,0:T(8,128)(2,1)}, bf16[256,1024]{1,0:T(...) fusion(bf16[256,8192]{1,0:T(8,128)(2,1)} %param.6, ...), kind=kLoop, calls=%fused_computation.9 | loop fusion | bytes 8388640 | tf_op jit(solution)/shard_map/dynamic_slice | solution.py:214
  11.4 3.6 %collective-permute-done.refs_3_ = bf16[256,1024]{1,0:T(8,128)(2,1)S(1)} collective-permute-done((bf16[256,1024]{1,0:T(8,128)(2,1)}, bf16[256,1024]{1,0:T(8,128)(2,1)S(1)}, u32[]{:S(2)}, u32[]{:S(2)}) %collective-permute-start) | collective-permute-done | bytes 524320 | tf_op jit(solution)/shard_map/ppermute | solution.py:216
  15.0 2.3 %collective-permute-done.1.refs_5_.right = bf16[256,1024]{1,0:T(8,128)(2,1)S(1)} collective-permute-done((bf16[256,1024]{1,0:T(8,128)(2,1)}, bf16[256,1024]{1,0:T(8,128)(2,1)S(1)}, u32[]{:S(2)}, u32[]{:S(2)}) %collective-permute-start.1) | collective-permute-done | bytes 524320 | tf_op jit(solution)/shard_map/ppermute | solution.py:217
  17.3 2.3 %collective-permute-start.7 = (bf16[512,1024]{1,0:T(8,128)(2,1)S(1)}, bf16[512,1024]{1,0:T(8,128)(2,1)}, u32[]{:S(2)}, u32[]{:S(2)}) collective-permute-start(bf16[512,1024]{1,0:T(8,128)(2,1)S(1)} %constant_dynamic-slice_fusion.8), channel_id=1, source_target_pairs={{0,4},{8,76},{4,0},{12,72},{64,68},{72,12},{68,64},{76,8},{1,5},{9... | collective-permute-start | bytes 3145736 | tf_op jit(solution)/shard_map/ppermute | solution.py:234
  20.5 1.8 collective-permute-start.6
  22.4 2.7 %collective-permute-start.4 = (bf16[128,1024]{1,0:T(8,128)(2,1)S(1)}, bf16[128,1024]{1,0:T(8,128)(2,1)S(1)}, u32[]{:S(2)}, u32[]{:S(2)}) collective-permute-start(bf16[128,1024]{1,0:T(8,128)(2,1)S(1)} %slice.7), channel_id=1, source_target_pairs={{0,3},{1,0},{2,1},{3,2},{4,7},{5,4},{6,5},{7,6},{8,11},{9,8},{10,9... | collective-permute-start | bytes 786440 | tf_op jit(solution)/shard_map/ppermute | solution.py:231
  25.2 15.0 %collective-permute-done.3.far_a.refs_7_ = bf16[128,1024]{1,0:T(8,128)(2,1)S(1)} collective-permute-done((bf16[128,1024]{1,0:T(8,128)(2,1)S(1)}, bf16[128,1024]{1,0:T(8,128)(2,1)S(1)}, u32[]{:S(2)}, u32[]{:S(2)}) %collective-permute-start.3) | collective-permute-done | bytes 262176 | tf_op jit(solution)/shard_map/ppermute | solution.py:230
  41.7 2.7 %collective-permute-start.15 = (bf16[256,1024]{1,0:T(8,128)(2,1)}, bf16[256,1024]{1,0:T(8,128)(2,1)}, u32[]{:S(2)}, u32[]{:S(2)}) collective-permute-start(bf16[256,1024]{1,0:T(8,128)(2,1)} %get-tuple-element.56), channel_id=1, source_target_pairs={{1,0},{2,1},{3,2},{0,3},{5,4},{6,5},{7,6},{4,7},{9,8},{10,9},{11,1... | collective-permute-start | bytes 1572872 | tf_op jit(solution)/shard_map/ppermute | solution.py:227
  44.3 1.6 collective-permute-start.11
  46.0 6.8 %shard_map.93.refs_6_ = f32[1024,1024]{1,0:T(8,128)} custom-call(bf16[256,1024]{1,0:T(8,128)(2,1)} %get-tuple-element.58.f, bf16[256,1024]{1,0:T(8,128)(2,1)} %own.1, f32[1024,1024]{1,0:T(8,128)} %bitcast.42, f32[1024,1024]{1,0:T(8,128)} %bitcast.43), custom_call_target="tpu_custom_call" | custom-call | flops 536870912 | bytes 13631488 | tf_op jit(solution)/shard_map/pallas_call | solution.py:70
  52.8 1.8 collective-permute-done.14.refs_0_
  54.6 3.1 %collective-permute-start.8 = (bf16[256,1024]{1,0:T(8,128)(2,1)}, bf16[256,1024]{1,0:T(8,128)(2,1)S(1)}, u32[]{:S(2)}, u32[]{:S(2)}) collective-permute-start(bf16[256,1024]{1,0:T(8,128)(2,1)} %get-tuple-element.49), channel_id=1, source_target_pairs={{5,0},{6,1},{7,2},{4,3},{1,4},{2,5},{3,6},{0,7},{13,8},{14,9},{15,... | collective-permute-start | bytes 1572872 | tf_op jit(solution)/shard_map/ppermute | solution.py:227
  57.7 8.3 %collective-permute-done.15.refs_1_ = bf16[256,1024]{1,0:T(8,128)(2,1)} collective-permute-done((bf16[256,1024]{1,0:T(8,128)(2,1)}, bf16[256,1024]{1,0:T(8,128)(2,1)}, u32[]{:S(2)}, u32[]{:S(2)}) %collective-permute-start.15) | collective-permute-done | bytes 524320 | tf_op jit(solution)/shard_map/ppermute | solution.py:227
  66.1 3.4 %collective-permute-done.16.refs_2_ = bf16[256,1024]{1,0:T(8,128)(2,1)} collective-permute-done((bf16[256,1024]{1,0:T(8,128)(2,1)}, bf16[256,1024]{1,0:T(8,128)(2,1)}, u32[]{:S(2)}, u32[]{:S(2)}) %collective-permute-start.16) | collective-permute-done | bytes 524320 | tf_op jit(solution)/shard_map/ppermute | solution.py:227
  69.5 2.1 %collective-permute-start.10 = (bf16[256,1024]{1,0:T(8,128)(2,1)}, bf16[256,1024]{1,0:T(8,128)(2,1)S(1)}, u32[]{:S(2)}, u32[]{:S(2)}) collective-permute-start(bf16[256,1024]{1,0:T(8,128)(2,1)} %get-tuple-element.51), channel_id=1, source_target_pairs={{2,0},{3,1},{0,2},{1,3},{6,4},{7,5},{4,6},{5,7},{10,8},{11,9},{8,1... | collective-permute-start | bytes 1572872 | tf_op jit(solution)/shard_map/ppermute | solution.py:227
  71.6 6.9 %shard_map.94.refs_11_ = f32[1024,1024]{1,0:T(8,128)} custom-call(bf16[256,1024]{1,0:T(8,128)(2,1)} %collective-permute-done.14.refs_0_, bf16[256,1024]{1,0:T(8,128)(2,1)} %collective-permute-done.15.refs_1_, bf16[256,1024]{1,0:T(8,128)(2,1)} %collective-permute-done.16.refs_2_, bf16[256,1024]{1,0:T(8,128)(2,1)} %copy-done.5, bf16[256,1024]{1,0:T(8,128)(2,1)} %copy-done.1, ...), custom_call_target="tpu_custom_call" | custom-call | flops 1610612736 | bytes 11534336 | tf_op jit(solution)/shard_map/pallas_call | solution.py:70
  80.1 9.7 %back.1 = (bf16[2,256,1024]{2,1,0:T(8,128)(2,1)}, bf16[2,256,1024]{2,1,0:T(8,128)(2,1)}, bf16[2,256,1024]{2,1,0:T(8,128)(2,1)}, bf16[2,256,1024]{2,1,0:T(8,128)(2,1)}) custom-call(s32[1]{0:T(128)} %bitcast.14.core_ref.refs_0_, bf16[256,1024]{1,0:T(8,128)(2,1)} %own.1, bf16[256,1024]{1,0:T(8,128)(2,1)} %copy-done.1, bf16[256,1024]{1,0:T(8,128)(2,1)} %copy-done, ...), custom_call_target="tpu_custom_call" | custom-call | flops 4294967296 | bytes 10485760 | tf_op jit(solution)/shard_map/back/pallas_call | solution.py:153
  89.7 8.3 %collective-permute-done.12.refs_9_ = bf16[128,1024]{1,0:T(8,128)(2,1)S(1)} collective-permute-done((bf16[128,1024]{1,0:T(8,128)(2,1)S(1)}, bf16[128,1024]{1,0:T(8,128)(2,1)S(1)}, u32[]{:S(2)}, u32[]{:S(2)}) %collective-permute-start.12) | collective-permute-done | bytes 262176 | tf_op jit(solution)/shard_map/ppermute | solution.py:243
  98.0 5.6 %collective-permute-done.13.refs_10_ = bf16[128,1024]{1,0:T(8,128)(2,1)S(1)} collective-permute-done((bf16[128,1024]{1,0:T(8,128)(2,1)S(1)}, bf16[128,1024]{1,0:T(8,128)(2,1)S(1)}, u32[]{:S(2)}, u32[]{:S(2)}) %collective-permute-start.13) | collective-permute-done | bytes 262176 | tf_op jit(solution)/shard_map/ppermute | solution.py:244
  104.9 9.4 %late.1 = (f32[1024,1024]{1,0:T(8,128)}, bf16[8,64,1024]{2,1,0:T(8,128)(2,1)}, bf16[8,64,1024]{2,1,0:T(8,128)(2,1)}) custom-call(s32[1]{0:T(128)} %bitcast.14.core_ref.refs_0_, bf16[256,1024]{1,0:T(8,128)(2,1)} %copy-done.9, bf16[256,1024]{1,0:T(8,128)(2,1)} %copy-done.10, bf16[256,1024]{1,0:T(8,128)(2,1)} %copy-done.11, bf16[256,1024]{1,0:T(8,128)(2,1)} %copy-done.8, ...), custom_call_target="tpu_custom_call" | custom-call | flops 2147483648 | bytes 14680064 | tf_op jit(solution)/shard_map/late/pallas_call | solution.py:113
  115.0 2.5 %collective-permute-done.21 = bf16[8,64,1024]{2,1,0:T(8,128)(2,1)S(1)} collective-permute-done((bf16[8,64,1024]{2,1,0:T(8,128)(2,1)}, bf16[8,64,1024]{2,1,0:T(8,128)(2,1)S(1)}, u32[]{:S(2)}, u32[]{:S(2)}) %collective-permute-start.21) | collective-permute-done | bytes 1048608 | tf_op jit(solution)/shard_map/ppermute | solution.py:267
  117.5 1.6 add_convert_fusion
  119.2 21.5 %all_to_all.10 = bf16[8,64,1024]{2,1,0:T(8,128)(2,1)S(1)} all-to-all(bf16[8,64,1024]{2,1,0:T(8,128)(2,1)S(1)} %add_convert_fusion), channel_id=1, replica_groups=mesh['zh'=2,'x'=4,'core'=2,'zl'=2,'y'=4] {'zh','x'}, dimensions={0} | all-to-all | bytes 2097152 | tf_op jit(solution)/shard_map/all_to_all | solution.py:269
  142.9 3.6 %all-to-all-start.1 = ((bf16[8,64,1024]{2,1,0:T(8,128)(2,1)}), bf16[8,64,1024]{2,1,0:T(8,128)(2,1)S(1)}, u32[]{:S(2)}, u32[]{:S(2)}) async-start(bf16[8,64,1024]{2,1,0:T(8,128)(2,1)} %broadcast_in_dim.36), calls=%async_computation.1 | async-start | bytes 2097152 | tf_op jit(solution)/shard_map/all_to_all | solution.py:274
  146.6 2.7 %collective-permute-start.19 = (bf16[2,256,1024]{2,1,0:T(8,128)(2,1)}, bf16[2,256,1024]{2,1,0:T(8,128)(2,1)S(1)}, u32[]{:S(2)}, u32[]{:S(2)}) collective-permute-start(bf16[2,256,1024]{2,1,0:T(8,128)(2,1)} %get-tuple-element.66), channel_id=1, source_target_pairs={{0,3},{1,0},{2,1},{3,2},{4,7},{5,4},{6,5},{7,6},{8,11},{9,8},{10,9... | collective-permute-start | bytes 3145736 | tf_op jit(solution)/shard_map/ppermute | solution.py:261
  149.7 14.1 %all-to-all-done.1 = bf16[8,64,1024]{2,1,0:T(8,128)(2,1)S(1)} async-done(((bf16[8,64,1024]{2,1,0:T(8,128)(2,1)}), bf16[8,64,1024]{2,1,0:T(8,128)(2,1)S(1)}, u32[]{:S(2)}, u32[]{:S(2)}) %all-to-all-start.1) | async-done | bytes 1048608 | tf_op jit(solution)/shard_map/all_to_all | solution.py:274
  165.5 6.1 %collective-permute-done.18.refs_1_ = bf16[2,256,1024]{2,1,0:T(8,128)(2,1)S(1)} collective-permute-done((bf16[2,256,1024]{2,1,0:T(8,128)(2,1)}, bf16[2,256,1024]{2,1,0:T(8,128)(2,1)S(1)}, u32[]{:S(2)}, u32[]{:S(2)}) %collective-permute-start.18) | collective-permute-done | bytes 1048608 | tf_op jit(solution)/shard_map/ppermute | solution.py:260
  171.6 22.4 %collective-permute-done.20.refs_3_ = bf16[2,256,1024]{2,1,0:T(8,128)(2,1)} collective-permute-done((bf16[2,256,1024]{2,1,0:T(8,128)(2,1)}, bf16[2,256,1024]{2,1,0:T(8,128)(2,1)}, u32[]{:S(2)}, u32[]{:S(2)}) %collective-permute-start.20) | collective-permute-done | bytes 1048608 | tf_op jit(solution)/shard_map/ppermute | solution.py:262
  194.0 4.0 %place.1 = bf16[256,8192]{1,0:T(8,128)(2,1)} custom-call(s32[4,2]{1,0:T(4,128)} %pad_add_fusion.at_ref, bf16[2,256,1024]{2,1,0:T(8,128)(2,1)} %get-tuple-element.64.refs_0_, bf16[2,256,1024]{2,1,0:T(8,128)(2,1)} %copy-done.2, bf16[2,256,1024]{2,1,0:T(8,128)(2,1)} %copy-done.3, bf16[2,256,1024]{2,1,0:T(8,128)(2,1)} %collective-permute-done.20.refs_3_), custom_call_target="tpu_custom_call" | custom-call | bytes 8388608 | tf_op jit(solution)/shard_map/place/pallas_call | solution.py:191
  198.0 2.8 %bitcast_select_fusion = bf16[1024,1024]{1,0:T(8,128)(2,1)} fusion(pred[1024]{0:T(1024)(128)(4,1)S(1)} %iota.12, bf16[8,64,1024]{2,1,0:T(8,128)(2,1)} %collective-permute-done.22, bf16[8,64,1024]{2,1,0:T(8,128)(2,1)S(1)} %all-to-all-done.1), kind=kLoop, calls=%fused_computation | loop fusion | flops 1048576 | bytes 4195328 | tf_op jit(solution)/shard_map/jit(_where)/select_n | solution.py:277
  (73 shorter events, 13.0 us)
Async XLA Ops:
  0.6 14.4 %collective-permute-start = (bf16[256,1024]{1,0:T(8,128)(2,1)}, bf16[256,1024]{1,0:T(8,128)(2,1)S(1)}, u32[]{:S(2)}, u32[]{:S(2)}) collective-permute-start(bf16[256,1024]{1,0:T(8,128)(2,1)} %own.1), channel_id=1, source_target_pairs={{0,4},{4,0},{1,5},{5,1},{2,6},{6,2},{3,7},{7,3},{8,12},{12,8},{9,1... | collective-permute-start | bytes 1572872 | tf_op jit(solution)/shard_map/ppermute | solution.py:216
  3.2 14.1 %collective-permute-start.1 = (bf16[256,1024]{1,0:T(8,128)(2,1)}, bf16[256,1024]{1,0:T(8,128)(2,1)S(1)}, u32[]{:S(2)}, u32[]{:S(2)}) collective-permute-start(bf16[256,1024]{1,0:T(8,128)(2,1)} %own.1), channel_id=1, source_target_pairs={{0,1},{1,2},{2,3},{3,0},{4,5},{5,6},{6,7},{7,4},{8,9},{9,10},{10,1... | collective-permute-start | bytes 1572872 | tf_op jit(solution)/shard_map/ppermute | solution.py:217
  4.5 12.8 %collective-permute-start.2 = (bf16[256,1024]{1,0:T(8,128)(2,1)}, bf16[256,1024]{1,0:T(8,128)(2,1)S(1)}, u32[]{:S(2)}, u32[]{:S(2)}) collective-permute-start(bf16[256,1024]{1,0:T(8,128)(2,1)} %own.1), channel_id=1, source_target_pairs={{0,3},{1,0},{2,1},{3,2},{4,7},{5,4},{6,5},{7,6},{8,11},{9,8},{10,9... | collective-permute-start | bytes 1572872 | tf_op jit(solution)/shard_map/ppermute | solution.py:218
  15.0 37.8 %copy-start.5 = (bf16[256,1024]{1,0:T(8,128)(2,1)}, bf16[256,1024]{1,0:T(8,128)(2,1)S(1)}, u32[]{:S(2)}) copy-start(bf16[256,1024]{1,0:T(8,128)(2,1)S(1)} %collective-permute-done.refs_3_) | copy-start | bytes 1572868
  17.3 35.5 %copy-start = (bf16[256,1024]{1,0:T(8,128)(2,1)}, bf16[256,1024]{1,0:T(8,128)(2,1)S(1)}, u32[]{:S(2)}) copy-start(bf16[256,1024]{1,0:T(8,128)(2,1)S(1)} %collective-permute-done.1.refs_5_.right) | copy-start | bytes 1572868
  17.3 35.5 %copy-start.1 = (bf16[256,1024]{1,0:T(8,128)(2,1)}, bf16[256,1024]{1,0:T(8,128)(2,1)S(1)}, u32[]{:S(2)}) copy-start(bf16[256,1024]{1,0:T(8,128)(2,1)S(1)} %collective-permute-done.2.refs_4_.left) | copy-start | bytes 1572868
  17.3 22.9 %collective-permute-start.7 = (bf16[512,1024]{1,0:T(8,128)(2,1)S(1)}, bf16[512,1024]{1,0:T(8,128)(2,1)}, u32[]{:S(2)}, u32[]{:S(2)}) collective-permute-start(bf16[512,1024]{1,0:T(8,128)(2,1)S(1)} %constant_dynamic-slice_fusion.8), channel_id=1, source_target_pairs={{0,4},{8,76},{4,0},{12,72},{64,68},{72,12},{68,64},{76,8},{1,5},{9... | collective-permute-start | bytes 3145736 | tf_op jit(solution)/shard_map/ppermute | solution.py:234
  19.6 20.5 %collective-permute-start.5 = (bf16[256,1024]{1,0:T(8,128)(2,1)S(1)}, bf16[256,1024]{1,0:T(8,128)(2,1)S(1)}, u32[]{:S(2)}, u32[]{:S(2)}) collective-permute-start(bf16[256,1024]{1,0:T(8,128)(2,1)S(1)} %collective-permute-done.refs_3_), channel_id=1, source_target_pairs={{0,1},{1,2},{2,3},{3,0},{4,5},{5,6},{6,7},{7,4},{8,9},{9,10},{10,1... | collective-permute-start | bytes 1572872 | tf_op jit(solution)/shard_map/ppermute | solution.py:232
  20.5 19.7 %collective-permute-start.6 = (bf16[256,1024]{1,0:T(8,128)(2,1)S(1)}, bf16[256,1024]{1,0:T(8,128)(2,1)S(1)}, u32[]{:S(2)}, u32[]{:S(2)}) collective-permute-start(bf16[256,1024]{1,0:T(8,128)(2,1)S(1)} %collective-permute-done.refs_3_), channel_id=1, source_target_pairs={{0,3},{1,0},{2,1},{3,2},{4,7},{5,4},{6,5},{7,6},{8,11},{9,8},{10,9... | collective-permute-start | bytes 1572872 | tf_op jit(solution)/shard_map/ppermute | solution.py:233
  22.3 17.8 %collective-permute-start.3 = (bf16[128,1024]{1,0:T(8,128)(2,1)S(1)}, bf16[128,1024]{1,0:T(8,128)(2,1)S(1)}, u32[]{:S(2)}, u32[]{:S(2)}) collective-permute-start(bf16[128,1024]{1,0:T(8,128)(2,1)S(1)} %slice.6), channel_id=1, source_target_pairs={{0,1},{1,2},{2,3},{3,0},{4,5},{5,6},{6,7},{7,4},{8,9},{9,10},{10,1... | collective-permute-start | bytes 786440 | tf_op jit(solution)/shard_map/ppermute | solution.py:230
  22.4 17.7 %collective-permute-start.4 = (bf16[128,1024]{1,0:T(8,128)(2,1)S(1)}, bf16[128,1024]{1,0:T(8,128)(2,1)S(1)}, u32[]{:S(2)}, u32[]{:S(2)}) collective-permute-start(bf16[128,1024]{1,0:T(8,128)(2,1)S(1)} %slice.7), channel_id=1, source_target_pairs={{0,3},{1,0},{2,1},{3,2},{4,7},{5,4},{6,5},{7,6},{8,11},{9,8},{10,9... | collective-permute-start | bytes 786440 | tf_op jit(solution)/shard_map/ppermute | solution.py:231
  40.1 38.4 %copy-start.12 = (bf16[128,1024]{1,0:T(8,128)(2,1)}, bf16[128,1024]{1,0:T(8,128)(2,1)S(1)}, u32[]{:S(2)}) copy-start(bf16[128,1024]{1,0:T(8,128)(2,1)S(1)} %collective-permute-done.3.far_a.refs_7_) | copy-start | bytes 786436
  40.2 39.2 %collective-permute-start.17 = (bf16[512,1024]{1,0:T(8,128)(2,1)}, bf16[512,1024]{1,0:T(8,128)(2,1)}, u32[]{:S(2)}, u32[]{:S(2)}) collective-permute-start(bf16[512,1024]{1,0:T(8,128)(2,1)} %collective-permute-done.7.got), channel_id=1, source_target_pairs={{0,8},{8,0},{1,9},{9,1},{2,10},{10,2},{3,11},{11,3},{4,12},{12,4},... | collective-permute-start | bytes 3145736 | tf_op jit(solution)/shard_map/ppermute | solution.py:248
  40.9 13.7 %collective-permute-start.14 = (bf16[256,1024]{1,0:T(8,128)(2,1)}, bf16[256,1024]{1,0:T(8,128)(2,1)}, u32[]{:S(2)}, u32[]{:S(2)}) collective-permute-start(bf16[256,1024]{1,0:T(8,128)(2,1)} %get-tuple-element.55), channel_id=1, source_target_pairs={{4,0},{5,1},{6,2},{7,3},{0,4},{1,5},{2,6},{3,7},{12,8},{13,9},{14,... | collective-permute-start | bytes 1572872 | tf_op jit(solution)/shard_map/ppermute | solution.py:227
  41.7 24.4 %collective-permute-start.15 = (bf16[256,1024]{1,0:T(8,128)(2,1)}, bf16[256,1024]{1,0:T(8,128)(2,1)}, u32[]{:S(2)}, u32[]{:S(2)}) collective-permute-start(bf16[256,1024]{1,0:T(8,128)(2,1)} %get-tuple-element.56), channel_id=1, source_target_pairs={{1,0},{2,1},{3,2},{0,3},{5,4},{6,5},{7,6},{4,7},{9,8},{10,9},{11,1... | collective-permute-start | bytes 1572872 | tf_op jit(solution)/shard_map/ppermute | solution.py:227
  44.3 25.2 %collective-permute-start.16 = (bf16[256,1024]{1,0:T(8,128)(2,1)}, bf16[256,1024]{1,0:T(8,128)(2,1)}, u32[]{:S(2)}, u32[]{:S(2)}) collective-permute-start(bf16[256,1024]{1,0:T(8,128)(2,1)} %get-tuple-element.57), channel_id=1, source_target_pairs={{3,0},{0,1},{1,2},{2,3},{7,4},{4,5},{5,6},{6,7},{11,8},{8,9},{9,10... | collective-permute-start | bytes 1572872 | tf_op jit(solution)/shard_map/ppermute | solution.py:227
  44.3 34.2 %collective-permute-start.11 = (bf16[256,1024]{1,0:T(8,128)(2,1)}, bf16[256,1024]{1,0:T(8,128)(2,1)S(1)}, u32[]{:S(2)}, u32[]{:S(2)}) collective-permute-start(bf16[256,1024]{1,0:T(8,128)(2,1)} %get-tuple-element.52), channel_id=1, source_target_pairs={{6,0},{7,1},{4,2},{5,3},{2,4},{3,5},{0,6},{1,7},{14,8},{15,9},{12,... | collective-permute-start | bytes 1572872 | tf_op jit(solution)/shard_map/ppermute | solution.py:227
  54.6 24.7 %copy-start.14 = (bf16[128,1024]{1,0:T(8,128)(2,1)S(1)}, bf16[128,1024]{1,0:T(8,128)(2,1)}, u32[]{:S(2)}) copy-start(bf16[128,1024]{1,0:T(8,128)(2,1)} %copy-done.13) | copy-start | bytes 786436
  54.6 49.0 %collective-permute-start.8 = (bf16[256,1024]{1,0:T(8,128)(2,1)}, bf16[256,1024]{1,0:T(8,128)(2,1)S(1)}, u32[]{:S(2)}, u32[]{:S(2)}) collective-permute-start(bf16[256,1024]{1,0:T(8,128)(2,1)} %get-tuple-element.49), channel_id=1, source_target_pairs={{5,0},{6,1},{7,2},{4,3},{1,4},{2,5},{3,6},{0,7},{13,8},{14,9},{15,... | collective-permute-start | bytes 1572872 | tf_op jit(solution)/shard_map/ppermute | solution.py:227
  66.1 37.5 %collective-permute-start.9 = (bf16[256,1024]{1,0:T(8,128)(2,1)}, bf16[256,1024]{1,0:T(8,128)(2,1)S(1)}, u32[]{:S(2)}, u32[]{:S(2)}) collective-permute-start(bf16[256,1024]{1,0:T(8,128)(2,1)} %get-tuple-element.50), channel_id=1, source_target_pairs={{7,0},{4,1},{5,2},{6,3},{3,4},{0,5},{1,6},{2,7},{15,8},{12,9},{13,... | collective-permute-start | bytes 1572872 | tf_op jit(solution)/shard_map/ppermute | solution.py:227
  69.5 34.1 %collective-permute-start.10 = (bf16[256,1024]{1,0:T(8,128)(2,1)}, bf16[256,1024]{1,0:T(8,128)(2,1)S(1)}, u32[]{:S(2)}, u32[]{:S(2)}) collective-permute-start(bf16[256,1024]{1,0:T(8,128)(2,1)} %get-tuple-element.51), channel_id=1, source_target_pairs={{2,0},{3,1},{0,2},{1,3},{6,4},{7,5},{4,6},{5,7},{10,8},{11,9},{8,1... | collective-permute-start | bytes 1572872 | tf_op jit(solution)/shard_map/ppermute | solution.py:227
  78.5 19.5 %collective-permute-start.12 = (bf16[128,1024]{1,0:T(8,128)(2,1)S(1)}, bf16[128,1024]{1,0:T(8,128)(2,1)S(1)}, u32[]{:S(2)}, u32[]{:S(2)}) collective-permute-start(bf16[128,1024]{1,0:T(8,128)(2,1)S(1)} %collective-permute-done.3.far_a.refs_7_), channel_id=1, source_target_pairs={{0,4},{4,0},{1,5},{5,1},{2,6},{6,2},{3,7},{7,3},{8,12},{12,8},{9,1... | collective-permute-start | bytes 786440 | tf_op jit(solution)/shard_map/ppermute | solution.py:243
  79.3 24.2 %collective-permute-start.13 = (bf16[128,1024]{1,0:T(8,128)(2,1)S(1)}, bf16[128,1024]{1,0:T(8,128)(2,1)S(1)}, u32[]{:S(2)}, u32[]{:S(2)}) collective-permute-start(bf16[128,1024]{1,0:T(8,128)(2,1)S(1)} %copy-done.14), channel_id=1, source_target_pairs={{0,4},{4,0},{1,5},{5,1},{2,6},{6,2},{3,7},{7,3},{8,12},{12,8},{9,1... | collective-permute-start | bytes 786440 | tf_op jit(solution)/shard_map/ppermute | solution.py:244
  114.3 3.2 %collective-permute-start.21 = (bf16[8,64,1024]{2,1,0:T(8,128)(2,1)}, bf16[8,64,1024]{2,1,0:T(8,128)(2,1)S(1)}, u32[]{:S(2)}, u32[]{:S(2)}) collective-permute-start(bf16[8,64,1024]{2,1,0:T(8,128)(2,1)} %get-tuple-element.78), channel_id=1, source_target_pairs={{0,8},{8,0},{1,9},{9,1},{2,10},{10,2},{3,11},{11,3},{4,12},{12,4},... | collective-permute-start | bytes 3145736 | tf_op jit(solution)/shard_map/ppermute | solution.py:267
  119.2 21.7 %copy-start.4 = (f32[1,64,1024]{2,1,0:T(8,128)S(1)}, f32[1,64,1024]{2,1,0:T(8,128)}, u32[]{:S(2)}) copy-start(f32[1,64,1024]{2,1,0:T(8,128)} %param.11) | copy-start | bytes 786436
  142.9 20.9 %all-to-all-start.1 = ((bf16[8,64,1024]{2,1,0:T(8,128)(2,1)}), bf16[8,64,1024]{2,1,0:T(8,128)(2,1)S(1)}, u32[]{:S(2)}, u32[]{:S(2)}) async-start(bf16[8,64,1024]{2,1,0:T(8,128)(2,1)} %broadcast_in_dim.36), calls=%async_computation.1 | async-start | bytes 2097152 | tf_op jit(solution)/shard_map/all_to_all | solution.py:274
  146.5 25.1 %collective-permute-start.18 = (bf16[2,256,1024]{2,1,0:T(8,128)(2,1)}, bf16[2,256,1024]{2,1,0:T(8,128)(2,1)S(1)}, u32[]{:S(2)}, u32[]{:S(2)}) collective-permute-start(bf16[2,256,1024]{2,1,0:T(8,128)(2,1)} %get-tuple-element.65), channel_id=1, source_target_pairs={{0,1},{1,2},{2,3},{3,0},{4,5},{5,6},{6,7},{7,4},{8,9},{9,10},{10,1... | collective-permute-start | bytes 3145736 | tf_op jit(solution)/shard_map/ppermute | solution.py:260
  146.6 25.0 %collective-permute-start.19 = (bf16[2,256,1024]{2,1,0:T(8,128)(2,1)}, bf16[2,256,1024]{2,1,0:T(8,128)(2,1)S(1)}, u32[]{:S(2)}, u32[]{:S(2)}) collective-permute-start(bf16[2,256,1024]{2,1,0:T(8,128)(2,1)} %get-tuple-element.66), channel_id=1, source_target_pairs={{0,3},{1,0},{2,1},{3,2},{4,7},{5,4},{6,5},{7,6},{8,11},{9,8},{10,9... | collective-permute-start | bytes 3145736 | tf_op jit(solution)/shard_map/ppermute | solution.py:261
  149.3 44.7 %collective-permute-start.20 = (bf16[2,256,1024]{2,1,0:T(8,128)(2,1)}, bf16[2,256,1024]{2,1,0:T(8,128)(2,1)}, u32[]{:S(2)}, u32[]{:S(2)}) collective-permute-start(bf16[2,256,1024]{2,1,0:T(8,128)(2,1)} %get-tuple-element.67), channel_id=1, source_target_pairs={{0,2},{1,3},{2,0},{3,1},{4,6},{5,7},{6,4},{7,5},{8,10},{9,11},{10,... | collective-permute-start | bytes 3145736 | tf_op jit(solution)/shard_map/ppermute | solution.py:262
  163.8 34.2 %collective-permute-start.22 = (bf16[8,64,1024]{2,1,0:T(8,128)(2,1)S(1)}, bf16[8,64,1024]{2,1,0:T(8,128)(2,1)}, u32[]{:S(2)}, u32[]{:S(2)}) collective-permute-start(bf16[8,64,1024]{2,1,0:T(8,128)(2,1)S(1)} %all-to-all-done.1), channel_id=1, source_target_pairs={{0,8},{8,0},{1,9},{9,1},{2,10},{10,2},{3,11},{11,3},{4,12},{12,4},... | collective-permute-start | bytes 3145736 | tf_op jit(solution)/shard_map/ppermute | solution.py:275
  171.6 22.4 %copy-start.2 = (bf16[2,256,1024]{2,1,0:T(8,128)(2,1)}, bf16[2,256,1024]{2,1,0:T(8,128)(2,1)S(1)}, u32[]{:S(2)}) copy-start(bf16[2,256,1024]{2,1,0:T(8,128)(2,1)S(1)} %collective-permute-done.18.refs_1_) | copy-start | bytes 3145732
  171.6 22.4 %copy-start.3 = (bf16[2,256,1024]{2,1,0:T(8,128)(2,1)}, bf16[2,256,1024]{2,1,0:T(8,128)(2,1)S(1)}, u32[]{:S(2)}) copy-start(bf16[2,256,1024]{2,1,0:T(8,128)(2,1)S(1)} %collective-permute-done.19.refs_2_) | copy-start | bytes 3145732
  (9 other events, 50.4 us)
where the time goes:
time: 203 us; the launch traced here: 201 us
  waiting for transfers between devices  93.4 us (46%)
  Pallas kernels  36.8 us (18%)
  starting transfers between devices  33.8 us (17%)
  blocking collectives  21.5 us (11%)
  local copies, waits for them, and re-layouts  8.12 us (4%)
  other arithmetic  6.27 us (3%)
    ppermute x1, waiting for transfers between devices, per_device(): home_2 = lax.ppermute(back_2, 'y', shift_y(2))  22.4 us
    all_to_all x1, blocking collectives, per_device(): parts = lax.all_to_all(pair, CHIPS, 0, 0)  21.5 us
    ppermute x1, waiting for transfers between devices, per_device(): far_a = lax.ppermute(k03[:TOK // 2], 'y', shift_y(1))  15 us
    all_to_all x1, waiting for transfers between devices, per_device(): lax.all_to_all(jnp.broadcast_to(block[None], (8, OWN, KV)), CHIPS, 0, 0)  14.1 us
    pallas_call x2, Pallas kernels, early_call(): pl.pallas_call(kernel, out_shape=jax.ShapeDtypeStruct((BLK, KV), jnp.floa...  13.8 us
    ppermute x7, waiting for transfers between devices, send(): return lax.ppermute(pieces[key], SHARD, shard_perm(*key))  13.5 us
    ppermute x7, starting transfers between devices, send(): return lax.ppermute(pieces[key], SHARD, shard_perm(*key))  10.2 us
    pallas_call x1, Pallas kernels, back_call(): pl.pallas_call(back_kernel, out_shape=(out,) * 4, grid_spec=pltpu.Prefetc...  9.65 us
  transfers between devices with their start and end apart: 24, of which 12 were waited for; matrix products, arithmetic and copies ran while one was open for 3% of the time, Pallas kernels for 14%

commit v1 on v0

--- a/solution.py
+++ b/solution.py
@@ -14,7 +14,7 @@
 OWN = 64
 SHARD = ("zl", "y")
 CHIPS = ("zh", "x")
-Z = ("zh", "core", "zl")
+Z = ("zh", "zl")
 SWAP = [(0, 1), (1, 0)]
 
 
@@ -32,14 +32,7 @@
 
 
 def z_perm():
-    pairs = []
-    for zh in range(2):
-        for zl in range(2):
-            z = zh * 2 + zl
-            other = (z + 1) % 4 if z % 2 == 1 else (z + 3) % 4
-            pairs.append(((zh * 2 + 0) * 2 + zl, (zh * 2 + 0) * 2 + (1 - zl)))
-            pairs.append(((zh * 2 + 1) * 2 + zl, ((other // 2) * 2 + 1) * 2 + other % 2))
-    return pairs
+    return [(z, (z + 1) % 4 if z % 2 else (z + 3) % 4) for z in range(4)]
 
 
 def contract_tokens(feats, keys):
@@ -217,11 +210,12 @@
     k03 = lax.ppermute(key_grads, "y", shift_y(1))
     k01 = lax.ppermute(key_grads, "y", shift_y(-1))
     half_weight = lax.dynamic_slice_in_dim(key_weight, core * (BLK // 2), BLK // 2, axis=0)
+    got = lax.ppermute(half_weight, Z, z_perm())
     order = [(0, 0), (1, 0), (0, 1), (0, 3), (1, 2), (1, 1), (1, 3), (0, 2)]
     pieces = {k: columns(*k) for k in order}
-    flat = fence((k10, k03, k01, half_weight) + tuple(pieces.values()))
-    k10, k03, k01, half_weight = flat[:4]
-    pieces = dict(zip(order, flat[4:]))
+    flat = fence((k10, k03, k01) + tuple(pieces.values()))
+    k10, k03, k01 = flat[:3]
+    pieces = dict(zip(order, flat[3:]))
 
     def send(key):
         return lax.ppermute(pieces[key], SHARD, shard_perm(*key))
@@ -231,7 +225,6 @@
     far_b = lax.ppermute(k01[TOK // 2 :], "y", shift_y(-1))
     k13 = lax.ppermute(k10, "y", shift_y(1))
     k11 = lax.ppermute(k10, "y", shift_y(-1))
-    got = lax.ppermute(half_weight, Z, z_perm())
     for key in order[1:5]:
         feats[key] = send(key)
 

time: 203 us -> 204 us (level)
  waiting for transfers between devices: 93.4 us -> 89.5 us
  blocking collectives: 21.5 us -> 23.8 us
    all_to_all x1, blocking collectives: 21.5 us -> 23.8 us  [per_device(): parts = lax.all_to_all(pair, CHIPS, 0, 0)]
    ppermute x1, waiting for transfers between devices: 3.56 us -> 1.35 us  [per_device(): k10 = lax.ppermute(key_grads, 'zl', SWAP)]
where the time goes in v1:
time: 204 us; the launch traced here: 201 us
  waiting for transfers between devices  89.5 us (44%)
  Pallas kernels  36.8 us (18%)
  starting transfers between devices  35.2 us (17%)
  blocking collectives  23.8 us (12%)
  local copies, waits for them, and re-layouts  8.97 us (4%)
  other arithmetic  6.31 us (3%)
    all_to_all x1, blocking collectives, per_device(): parts = lax.all_to_all(pair, CHIPS, 0, 0)  23.8 us
    ppermute x1, waiting for transfers between devices, per_device(): home_2 = lax.ppermute(back_2, 'y', shift_y(2))  22.4 us
    all_to_all x1, waiting for transfers between devices, per_device(): lax.all_to_all(jnp.broadcast_to(block[None], (8, OWN, KV)), CHIPS, 0, 0)  14.2 us
    ppermute x7, waiting for transfers between devices, send(): return lax.ppermute(pieces[key], SHARD, shard_perm(*key))  13.9 us
    pallas_call x2, Pallas kernels, early_call(): pl.pallas_call(kernel, out_shape=jax.ShapeDtypeStruct((BLK, KV), jnp.floa...  13.7 us
    ppermute x1, waiting for transfers between devices, per_device(): far_a = lax.ppermute(k03[:TOK // 2], 'y', shift_y(1))  13.2 us
    ppermute x7, starting transfers between devices, send(): return lax.ppermute(pieces[key], SHARD, shard_perm(*key))  10.1 us
    pallas_call x1, Pallas kernels, back_call(): pl.pallas_call(back_kernel, out_shape=(out,) * 4, grid_spec=pltpu.Prefetc...  9.65 us
  transfers between devices with their start and end apart: 24, of which 12 were waited for; matrix products, arithmetic and copies ran while one was open for 3% of the time, Pallas kernels for 14%

profile of v1, /device:TPU:1, one launch (start us, length us, event | category | flops | bytes accessed | tf_op | source)
XLA Modules:
  0.0 201.5 jit_solution(11510531593573757726)
XLA Ops:
  0.6 2.5 %collective-permute-start = (bf16[256,1024]{1,0:T(8,128)(2,1)}, bf16[256,1024]{1,0:T(8,128)(2,1)S(1)}, u32[]{:S(2)}, u32[]{:S(2)}) collective-permute-start(bf16[256,1024]{1,0:T(8,128)(2,1)} %own.1), channel_id=1, source_target_pairs={{0,4},{4,0},{1,5},{5,1},{2,6},{6,2},{3,7},{7,3},{8,12},{12,8},{9,1... | collective-permute-start | bytes 1572872 | tf_op jit(solution)/shard_map/ppermute | solution.py:209
  4.5 1.4 collective-permute-start.2
  7.2 2.4 %collective-permute-start.7 = (bf16[512,1024]{1,0:T(8,128)(2,1)S(1)}, bf16[512,1024]{1,0:T(8,128)(2,1)}, u32[]{:S(2)}, u32[]{:S(2)}) collective-permute-start(bf16[512,1024]{1,0:T(8,128)(2,1)S(1)} %constant_dynamic-slice_fusion), channel_id=1, source_target_pairs={{0,68},{4,64},{64,4},{68,0},{1,69},{5,65},{65,5},{69,1},{2,70},{6,... | collective-permute-start | bytes 3145736 | tf_op jit(solution)/shard_map/ppermute | solution.py:213
  9.6 4.2 %constant_dynamic-slice_fusion.1 = (bf16[256,1024]{1,0:T(8,128)(2,1)}, bf16[256,1024]{1,0:T(8,128)(2,1)}, bf16[256,1024]{1,0:T(8,128)(2,1)}, bf16[256,1024]{1,0:...) fusion(bf16[256,8192]{1,0:T(8,128)(2,1)} %param.6, ...), kind=kLoop, calls=%fused_computation.10 | loop fusion | bytes 8388640 | tf_op jit(solution)/shard_map/dynamic_slice | solution.py:207
  15.1 2.3 %collective-permute-done.1.refs_5_.right = bf16[256,1024]{1,0:T(8,128)(2,1)S(1)} collective-permute-done((bf16[256,1024]{1,0:T(8,128)(2,1)}, bf16[256,1024]{1,0:T(8,128)(2,1)S(1)}, u32[]{:S(2)}, u32[]{:S(2)}) %collective-permute-start.1) | collective-permute-done | bytes 524320 | tf_op jit(solution)/shard_map/ppermute | solution.py:210
  18.3 1.8 collective-permute-start.6
  20.3 2.7 %collective-permute-start.4 = (bf16[128,1024]{1,0:T(8,128)(2,1)S(1)}, bf16[128,1024]{1,0:T(8,128)(2,1)S(1)}, u32[]{:S(2)}, u32[]{:S(2)}) collective-permute-start(bf16[128,1024]{1,0:T(8,128)(2,1)S(1)} %slice.7), channel_id=1, source_target_pairs={{0,3},{1,0},{2,1},{3,2},{4,7},{5,4},{6,5},{7,6},{8,11},{9,8},{10,9... | collective-permute-start | bytes 786440 | tf_op jit(solution)/shard_map/ppermute | solution.py:225
  23.0 13.2 %collective-permute-done.3.far_a.refs_7_ = bf16[128,1024]{1,0:T(8,128)(2,1)S(1)} collective-permute-done((bf16[128,1024]{1,0:T(8,128)(2,1)S(1)}, bf16[128,1024]{1,0:T(8,128)(2,1)S(1)}, u32[]{:S(2)}, u32[]{:S(2)}) %collective-permute-start.3) | collective-permute-done | bytes 262176 | tf_op jit(solution)/shard_map/ppermute | solution.py:224
  37.1 2.5 %collective-permute-start.17 = (bf16[512,1024]{1,0:T(8,128)(2,1)}, bf16[512,1024]{1,0:T(8,128)(2,1)}, u32[]{:S(2)}, u32[]{:S(2)}) collective-permute-start(bf16[512,1024]{1,0:T(8,128)(2,1)} %collective-permute-done.7.got), channel_id=1, source_target_pairs={{0,8},{8,0},{1,9},{9,1},{2,10},{10,2},{3,11},{11,3},{4,12},{12,4},... | collective-permute-start | bytes 3145736 | tf_op jit(solution)/shard_map/ppermute | solution.py:241
  39.8 2.6 %collective-permute-start.15 = (bf16[256,1024]{1,0:T(8,128)(2,1)}, bf16[256,1024]{1,0:T(8,128)(2,1)}, u32[]{:S(2)}, u32[]{:S(2)}) collective-permute-start(bf16[256,1024]{1,0:T(8,128)(2,1)} %get-tuple-element.54), channel_id=1, source_target_pairs={{1,0},{2,1},{3,2},{0,3},{5,4},{6,5},{7,6},{4,7},{9,8},{10,9},{11,1... | collective-permute-start | bytes 1572872 | tf_op jit(solution)/shard_map/ppermute | solution.py:221
  42.4 2.2 %collective-permute-start.11 = (bf16[256,1024]{1,0:T(8,128)(2,1)}, bf16[256,1024]{1,0:T(8,128)(2,1)S(1)}, u32[]{:S(2)}, u32[]{:S(2)}) collective-permute-start(bf16[256,1024]{1,0:T(8,128)(2,1)} %get-tuple-element.50), channel_id=1, source_target_pairs={{6,0},{7,1},{4,2},{5,3},{2,4},{3,5},{0,6},{1,7},{14,8},{15,9},{12,... | collective-permute-start | bytes 1572872 | tf_op jit(solution)/shard_map/ppermute | solution.py:221
  44.6 6.8 %shard_map.93.refs_6_ = f32[1024,1024]{1,0:T(8,128)} custom-call(bf16[256,1024]{1,0:T(8,128)(2,1)} %get-tuple-element.56.f, bf16[256,1024]{1,0:T(8,128)(2,1)} %own.1, f32[1024,1024]{1,0:T(8,128)} %bitcast.42, f32[1024,1024]{1,0:T(8,128)} %bitcast.43), custom_call_target="tpu_custom_call" | custom-call | flops 536870912 | bytes 13631488 | tf_op jit(solution)/shard_map/pallas_call | solution.py:63
  51.4 2.0 collective-permute-done.14.refs_0_
  53.4 2.5 %collective-permute-start.8 = (bf16[256,1024]{1,0:T(8,128)(2,1)}, bf16[256,1024]{1,0:T(8,128)(2,1)S(1)}, u32[]{:S(2)}, u32[]{:S(2)}) collective-permute-start(bf16[256,1024]{1,0:T(8,128)(2,1)} %get-tuple-element.47), channel_id=1, source_target_pairs={{5,0},{6,1},{7,2},{4,3},{1,4},{2,5},{3,6},{0,7},{13,8},{14,9},{15,... | collective-permute-start | bytes 1572872 | tf_op jit(solution)/shard_map/ppermute | solution.py:221
  55.9 8.4 %collective-permute-done.15.refs_1_ = bf16[256,1024]{1,0:T(8,128)(2,1)} collective-permute-done((bf16[256,1024]{1,0:T(8,128)(2,1)}, bf16[256,1024]{1,0:T(8,128)(2,1)}, u32[]{:S(2)}, u32[]{:S(2)}) %collective-permute-start.15) | collective-permute-done | bytes 524320 | tf_op jit(solution)/shard_map/ppermute | solution.py:221
  64.3 3.5 %collective-permute-done.16.refs_2_ = bf16[256,1024]{1,0:T(8,128)(2,1)} collective-permute-done((bf16[256,1024]{1,0:T(8,128)(2,1)}, bf16[256,1024]{1,0:T(8,128)(2,1)}, u32[]{:S(2)}, u32[]{:S(2)}) %collective-permute-start.16) | collective-permute-done | bytes 524320 | tf_op jit(solution)/shard_map/ppermute | solution.py:221
  67.8 2.6 %collective-permute-start.10 = (bf16[256,1024]{1,0:T(8,128)(2,1)}, bf16[256,1024]{1,0:T(8,128)(2,1)S(1)}, u32[]{:S(2)}, u32[]{:S(2)}) collective-permute-start(bf16[256,1024]{1,0:T(8,128)(2,1)} %get-tuple-element.49), channel_id=1, source_target_pairs={{2,0},{3,1},{0,2},{1,3},{6,4},{7,5},{4,6},{5,7},{10,8},{11,9},{8,1... | collective-permute-start | bytes 1572872 | tf_op jit(solution)/shard_map/ppermute | solution.py:221
  70.4 6.9 %shard_map.94.refs_11_ = f32[1024,1024]{1,0:T(8,128)} custom-call(bf16[256,1024]{1,0:T(8,128)(2,1)} %copy-done.12, bf16[256,1024]{1,0:T(8,128)(2,1)} %collective-permute-done.15.refs_1_, bf16[256,1024]{1,0:T(8,128)(2,1)} %collective-permute-done.16.refs_2_, bf16[256,1024]{1,0:T(8,128)(2,1)} %copy-done.5, bf16[256,1024]{1,0:T(8,128)(2,1)} %copy-done.1, ...), custom_call_target="tpu_custom_call" | custom-call | flops 1610612736 | bytes 11534336 | tf_op jit(solution)/shard_map/pallas_call | solution.py:63
  78.9 9.7 %back.1 = (bf16[2,256,1024]{2,1,0:T(8,128)(2,1)}, bf16[2,256,1024]{2,1,0:T(8,128)(2,1)}, bf16[2,256,1024]{2,1,0:T(8,128)(2,1)}, bf16[2,256,1024]{2,1,0:T(8,128)(2,1)}) custom-call(s32[1]{0:T(128)} %bitcast.14.core_ref.refs_0_, bf16[256,1024]{1,0:T(8,128)(2,1)} %own.1, bf16[256,1024]{1,0:T(8,128)(2,1)} %copy-done.1, bf16[256,1024]{1,0:T(8,128)(2,1)} %copy-done, ...), custom_call_target="tpu_custom_call" | custom-call | flops 4294967296 | bytes 10485760 | tf_op jit(solution)/shard_map/back/pallas_call | solution.py:146
  88.6 8.0 %collective-permute-done.12.refs_9_ = bf16[128,1024]{1,0:T(8,128)(2,1)S(1)} collective-permute-done((bf16[128,1024]{1,0:T(8,128)(2,1)S(1)}, bf16[128,1024]{1,0:T(8,128)(2,1)S(1)}, u32[]{:S(2)}, u32[]{:S(2)}) %collective-permute-start.12) | collective-permute-done | bytes 262176 | tf_op jit(solution)/shard_map/ppermute | solution.py:236
  96.6 5.6 %collective-permute-done.13.refs_10_ = bf16[128,1024]{1,0:T(8,128)(2,1)S(1)} collective-permute-done((bf16[128,1024]{1,0:T(8,128)(2,1)S(1)}, bf16[128,1024]{1,0:T(8,128)(2,1)S(1)}, u32[]{:S(2)}, u32[]{:S(2)}) %collective-permute-start.13) | collective-permute-done | bytes 262176 | tf_op jit(solution)/shard_map/ppermute | solution.py:237
  103.5 9.4 %late.1 = (f32[1024,1024]{1,0:T(8,128)}, bf16[8,64,1024]{2,1,0:T(8,128)(2,1)}, bf16[8,64,1024]{2,1,0:T(8,128)(2,1)}) custom-call(s32[1]{0:T(128)} %bitcast.14.core_ref.refs_0_, bf16[256,1024]{1,0:T(8,128)(2,1)} %copy-done.9, bf16[256,1024]{1,0:T(8,128)(2,1)} %copy-done.10, bf16[256,1024]{1,0:T(8,128)(2,1)} %copy-done.11, bf16[256,1024]{1,0:T(8,128)(2,1)} %copy-done.8, ...), custom_call_target="tpu_custom_call" | custom-call | flops 2147483648 | bytes 14680064 | tf_op jit(solution)/shard_map/late/pallas_call | solution.py:106
  113.4 2.5 %collective-permute-done.21 = bf16[8,64,1024]{2,1,0:T(8,128)(2,1)S(1)} collective-permute-done((bf16[8,64,1024]{2,1,0:T(8,128)(2,1)}, bf16[8,64,1024]{2,1,0:T(8,128)(2,1)S(1)}, u32[]{:S(2)}, u32[]{:S(2)}) %collective-permute-start.21) | collective-permute-done | bytes 1048608 | tf_op jit(solution)/shard_map/ppermute | solution.py:260
  115.9 1.6 add_convert_fusion
  117.6 23.8 %all_to_all.10 = bf16[8,64,1024]{2,1,0:T(8,128)(2,1)S(1)} all-to-all(bf16[8,64,1024]{2,1,0:T(8,128)(2,1)S(1)} %add_convert_fusion), channel_id=1, replica_groups=mesh['zh'=2,'x'=4,'core'=2,'zl'=2,'y'=4] {'zh','x'}, dimensions={0} | all-to-all | bytes 2097152 | tf_op jit(solution)/shard_map/all_to_all | solution.py:262
  143.6 3.6 %all-to-all-start.1 = ((bf16[8,64,1024]{2,1,0:T(8,128)(2,1)}), bf16[8,64,1024]{2,1,0:T(8,128)(2,1)S(1)}, u32[]{:S(2)}, u32[]{:S(2)}) async-start(bf16[8,64,1024]{2,1,0:T(8,128)(2,1)} %broadcast_in_dim.36), calls=%async_computation.1 | async-start | bytes 2097152 | tf_op jit(solution)/shard_map/all_to_all | solution.py:267
  147.3 2.7 %collective-permute-start.19 = (bf16[2,256,1024]{2,1,0:T(8,128)(2,1)}, bf16[2,256,1024]{2,1,0:T(8,128)(2,1)S(1)}, u32[]{:S(2)}, u32[]{:S(2)}) collective-permute-start(bf16[2,256,1024]{2,1,0:T(8,128)(2,1)} %get-tuple-element.64), channel_id=1, source_target_pairs={{0,3},{1,0},{2,1},{3,2},{4,7},{5,4},{6,5},{7,6},{8,11},{9,8},{10,9... | collective-permute-start | bytes 3145736 | tf_op jit(solution)/shard_map/ppermute | solution.py:254
  150.3 14.2 %all-to-all-done.1 = bf16[8,64,1024]{2,1,0:T(8,128)(2,1)S(1)} async-done(((bf16[8,64,1024]{2,1,0:T(8,128)(2,1)}), bf16[8,64,1024]{2,1,0:T(8,128)(2,1)S(1)}, u32[]{:S(2)}, u32[]{:S(2)}) %all-to-all-start.1) | async-done | bytes 1048608 | tf_op jit(solution)/shard_map/all_to_all | solution.py:267
  166.2 6.0 %collective-permute-done.18.refs_1_ = bf16[2,256,1024]{2,1,0:T(8,128)(2,1)S(1)} collective-permute-done((bf16[2,256,1024]{2,1,0:T(8,128)(2,1)}, bf16[2,256,1024]{2,1,0:T(8,128)(2,1)S(1)}, u32[]{:S(2)}, u32[]{:S(2)}) %collective-permute-start.18) | collective-permute-done | bytes 1048608 | tf_op jit(solution)/shard_map/ppermute | solution.py:253
  172.3 22.4 %collective-permute-done.20.refs_3_ = bf16[2,256,1024]{2,1,0:T(8,128)(2,1)} collective-permute-done((bf16[2,256,1024]{2,1,0:T(8,128)(2,1)}, bf16[2,256,1024]{2,1,0:T(8,128)(2,1)}, u32[]{:S(2)}, u32[]{:S(2)}) %collective-permute-start.20) | collective-permute-done | bytes 1048608 | tf_op jit(solution)/shard_map/ppermute | solution.py:255
  194.7 4.0 %place.1 = bf16[256,8192]{1,0:T(8,128)(2,1)} custom-call(s32[4,2]{1,0:T(4,128)} %pad_add_fusion.at_ref, bf16[2,256,1024]{2,1,0:T(8,128)(2,1)} %get-tuple-element.62.refs_0_, bf16[2,256,1024]{2,1,0:T(8,128)(2,1)} %copy-done.2, bf16[2,256,1024]{2,1,0:T(8,128)(2,1)} %copy-done.3, bf16[2,256,1024]{2,1,0:T(8,128)(2,1)} %collective-permute-done.20.refs_3_), custom_call_target="tpu_custom_call" | custom-call | bytes 8388608 | tf_op jit(solution)/shard_map/place/pallas_call | solution.py:184
  198.7 2.8 %bitcast_select_fusion = bf16[1024,1024]{1,0:T(8,128)(2,1)} fusion(pred[1024]{0:T(1024)(128)(4,1)S(1)} %iota.12, bf16[8,64,1024]{2,1,0:T(8,128)(2,1)} %collective-permute-done.22, bf16[8,64,1024]{2,1,0:T(8,128)(2,1)S(1)} %all-to-all-done.1), kind=kLoop, calls=%fused_computation | loop fusion | flops 1048576 | bytes 4195328 | tf_op jit(solution)/shard_map/jit(_where)/select_n | solution.py:270
  (75 shorter events, 13.8 us)
Async XLA Ops:
  0.6 14.5 %collective-permute-start = (bf16[256,1024]{1,0:T(8,128)(2,1)}, bf16[256,1024]{1,0:T(8,128)(2,1)S(1)}, u32[]{:S(2)}, u32[]{:S(2)}) collective-permute-start(bf16[256,1024]{1,0:T(8,128)(2,1)} %own.1), channel_id=1, source_target_pairs={{0,4},{4,0},{1,5},{5,1},{2,6},{6,2},{3,7},{7,3},{8,12},{12,8},{9,1... | collective-permute-start | bytes 1572872 | tf_op jit(solution)/shard_map/ppermute | solution.py:209
  3.2 14.2 %collective-permute-start.1 = (bf16[256,1024]{1,0:T(8,128)(2,1)}, bf16[256,1024]{1,0:T(8,128)(2,1)S(1)}, u32[]{:S(2)}, u32[]{:S(2)}) collective-permute-start(bf16[256,1024]{1,0:T(8,128)(2,1)} %own.1), channel_id=1, source_target_pairs={{0,1},{1,2},{2,3},{3,0},{4,5},{5,6},{6,7},{7,4},{8,9},{9,10},{10,1... | collective-permute-start | bytes 1572872 | tf_op jit(solution)/shard_map/ppermute | solution.py:210
  4.5 12.9 %collective-permute-start.2 = (bf16[256,1024]{1,0:T(8,128)(2,1)}, bf16[256,1024]{1,0:T(8,128)(2,1)S(1)}, u32[]{:S(2)}, u32[]{:S(2)}) collective-permute-start(bf16[256,1024]{1,0:T(8,128)(2,1)} %own.1), channel_id=1, source_target_pairs={{0,3},{1,0},{2,1},{3,2},{4,7},{5,4},{6,5},{7,6},{8,11},{9,8},{10,9... | collective-permute-start | bytes 1572872 | tf_op jit(solution)/shard_map/ppermute | solution.py:211
  7.2 29.0 %collective-permute-start.7 = (bf16[512,1024]{1,0:T(8,128)(2,1)S(1)}, bf16[512,1024]{1,0:T(8,128)(2,1)}, u32[]{:S(2)}, u32[]{:S(2)}) collective-permute-start(bf16[512,1024]{1,0:T(8,128)(2,1)S(1)} %constant_dynamic-slice_fusion), channel_id=1, source_target_pairs={{0,68},{4,64},{64,4},{68,0},{1,69},{5,65},{65,5},{69,1},{2,70},{6,... | collective-permute-start | bytes 3145736 | tf_op jit(solution)/shard_map/ppermute | solution.py:213
  15.1 36.3 %copy-start.5 = (bf16[256,1024]{1,0:T(8,128)(2,1)}, bf16[256,1024]{1,0:T(8,128)(2,1)S(1)}, u32[]{:S(2)}) copy-start(bf16[256,1024]{1,0:T(8,128)(2,1)S(1)} %collective-permute-done.refs_3_) | copy-start | bytes 1572868
  17.4 34.0 %copy-start = (bf16[256,1024]{1,0:T(8,128)(2,1)}, bf16[256,1024]{1,0:T(8,128)(2,1)S(1)}, u32[]{:S(2)}) copy-start(bf16[256,1024]{1,0:T(8,128)(2,1)S(1)} %collective-permute-done.1.refs_5_.right) | copy-start | bytes 1572868
  17.4 34.0 %copy-start.1 = (bf16[256,1024]{1,0:T(8,128)(2,1)}, bf16[256,1024]{1,0:T(8,128)(2,1)S(1)}, u32[]{:S(2)}) copy-start(bf16[256,1024]{1,0:T(8,128)(2,1)S(1)} %collective-permute-done.2.refs_4_.left) | copy-start | bytes 1572868
  17.4 18.8 %collective-permute-start.5 = (bf16[256,1024]{1,0:T(8,128)(2,1)S(1)}, bf16[256,1024]{1,0:T(8,128)(2,1)S(1)}, u32[]{:S(2)}, u32[]{:S(2)}) collective-permute-start(bf16[256,1024]{1,0:T(8,128)(2,1)S(1)} %collective-permute-done.refs_3_), channel_id=1, source_target_pairs={{0,1},{1,2},{2,3},{3,0},{4,5},{5,6},{6,7},{7,4},{8,9},{9,10},{10,1... | collective-permute-start | bytes 1572872 | tf_op jit(solution)/shard_map/ppermute | solution.py:226
  18.3 17.9 %collective-permute-start.6 = (bf16[256,1024]{1,0:T(8,128)(2,1)S(1)}, bf16[256,1024]{1,0:T(8,128)(2,1)S(1)}, u32[]{:S(2)}, u32[]{:S(2)}) collective-permute-start(bf16[256,1024]{1,0:T(8,128)(2,1)S(1)} %collective-permute-done.refs_3_), channel_id=1, source_target_pairs={{0,3},{1,0},{2,1},{3,2},{4,7},{5,4},{6,5},{7,6},{8,11},{9,8},{10,9... | collective-permute-start | bytes 1572872 | tf_op jit(solution)/shard_map/ppermute | solution.py:227
  20.2 16.0 %collective-permute-start.3 = (bf16[128,1024]{1,0:T(8,128)(2,1)S(1)}, bf16[128,1024]{1,0:T(8,128)(2,1)S(1)}, u32[]{:S(2)}, u32[]{:S(2)}) collective-permute-start(bf16[128,1024]{1,0:T(8,128)(2,1)S(1)} %slice.6), channel_id=1, source_target_pairs={{0,1},{1,2},{2,3},{3,0},{4,5},{5,6},{6,7},{7,4},{8,9},{9,10},{10,1... | collective-permute-start | bytes 786440 | tf_op jit(solution)/shard_map/ppermute | solution.py:224
  20.3 15.9 %collective-permute-start.4 = (bf16[128,1024]{1,0:T(8,128)(2,1)S(1)}, bf16[128,1024]{1,0:T(8,128)(2,1)S(1)}, u32[]{:S(2)}, u32[]{:S(2)}) collective-permute-start(bf16[128,1024]{1,0:T(8,128)(2,1)S(1)} %slice.7), channel_id=1, source_target_pairs={{0,3},{1,0},{2,1},{3,2},{4,7},{5,4},{6,5},{7,6},{8,11},{9,8},{10,9... | collective-permute-start | bytes 786440 | tf_op jit(solution)/shard_map/ppermute | solution.py:225
  36.2 41.2 %copy-start.13 = (bf16[128,1024]{1,0:T(8,128)(2,1)}, bf16[128,1024]{1,0:T(8,128)(2,1)S(1)}, u32[]{:S(2)}) copy-start(bf16[128,1024]{1,0:T(8,128)(2,1)S(1)} %collective-permute-done.3.far_a.refs_7_) | copy-start | bytes 786436
  37.1 40.5 %collective-permute-start.17 = (bf16[512,1024]{1,0:T(8,128)(2,1)}, bf16[512,1024]{1,0:T(8,128)(2,1)}, u32[]{:S(2)}, u32[]{:S(2)}) collective-permute-start(bf16[512,1024]{1,0:T(8,128)(2,1)} %collective-permute-done.7.got), channel_id=1, source_target_pairs={{0,8},{8,0},{1,9},{9,1},{2,10},{10,2},{3,11},{11,3},{4,12},{12,4},... | collective-permute-start | bytes 3145736 | tf_op jit(solution)/shard_map/ppermute | solution.py:241
  39.6 13.8 %collective-permute-start.14 = (bf16[256,1024]{1,0:T(8,128)(2,1)}, bf16[256,1024]{1,0:T(8,128)(2,1)S(1)}, u32[]{:S(2)}, u32[]{:S(2)}) collective-permute-start(bf16[256,1024]{1,0:T(8,128)(2,1)} %get-tuple-element.53), channel_id=1, source_target_pairs={{4,0},{5,1},{6,2},{7,3},{0,4},{1,5},{2,6},{3,7},{12,8},{13,9},{14,... | collective-permute-start | bytes 1572872 | tf_op jit(solution)/shard_map/ppermute | solution.py:221
  39.8 24.5 %collective-permute-start.15 = (bf16[256,1024]{1,0:T(8,128)(2,1)}, bf16[256,1024]{1,0:T(8,128)(2,1)}, u32[]{:S(2)}, u32[]{:S(2)}) collective-permute-start(bf16[256,1024]{1,0:T(8,128)(2,1)} %get-tuple-element.54), channel_id=1, source_target_pairs={{1,0},{2,1},{3,2},{0,3},{5,4},{6,5},{7,6},{4,7},{9,8},{10,9},{11,1... | collective-permute-start | bytes 1572872 | tf_op jit(solution)/shard_map/ppermute | solution.py:221
  42.4 25.4 %collective-permute-start.16 = (bf16[256,1024]{1,0:T(8,128)(2,1)}, bf16[256,1024]{1,0:T(8,128)(2,1)}, u32[]{:S(2)}, u32[]{:S(2)}) collective-permute-start(bf16[256,1024]{1,0:T(8,128)(2,1)} %get-tuple-element.55), channel_id=1, source_target_pairs={{3,0},{0,1},{1,2},{2,3},{7,4},{4,5},{5,6},{6,7},{11,8},{8,9},{9,10... | collective-permute-start | bytes 1572872 | tf_op jit(solution)/shard_map/ppermute | solution.py:221
  42.4 34.9 %collective-permute-start.11 = (bf16[256,1024]{1,0:T(8,128)(2,1)}, bf16[256,1024]{1,0:T(8,128)(2,1)S(1)}, u32[]{:S(2)}, u32[]{:S(2)}) collective-permute-start(bf16[256,1024]{1,0:T(8,128)(2,1)} %get-tuple-element.50), channel_id=1, source_target_pairs={{6,0},{7,1},{4,2},{5,3},{2,4},{3,5},{0,6},{1,7},{14,8},{15,9},{12,... | collective-permute-start | bytes 1572872 | tf_op jit(solution)/shard_map/ppermute | solution.py:221
  53.4 24.2 %copy-start.15 = (bf16[128,1024]{1,0:T(8,128)(2,1)S(1)}, bf16[128,1024]{1,0:T(8,128)(2,1)}, u32[]{:S(2)}) copy-start(bf16[128,1024]{1,0:T(8,128)(2,1)} %copy-done.14) | copy-start | bytes 786436
  53.4 48.8 %collective-permute-start.8 = (bf16[256,1024]{1,0:T(8,128)(2,1)}, bf16[256,1024]{1,0:T(8,128)(2,1)S(1)}, u32[]{:S(2)}, u32[]{:S(2)}) collective-permute-start(bf16[256,1024]{1,0:T(8,128)(2,1)} %get-tuple-element.47), channel_id=1, source_target_pairs={{5,0},{6,1},{7,2},{4,3},{1,4},{2,5},{3,6},{0,7},{13,8},{14,9},{15,... | collective-permute-start | bytes 1572872 | tf_op jit(solution)/shard_map/ppermute | solution.py:221
  64.3 37.9 %collective-permute-start.9 = (bf16[256,1024]{1,0:T(8,128)(2,1)}, bf16[256,1024]{1,0:T(8,128)(2,1)S(1)}, u32[]{:S(2)}, u32[]{:S(2)}) collective-permute-start(bf16[256,1024]{1,0:T(8,128)(2,1)} %get-tuple-element.48), channel_id=1, source_target_pairs={{7,0},{4,1},{5,2},{6,3},{3,4},{0,5},{1,6},{2,7},{15,8},{12,9},{13,... | collective-permute-start | bytes 1572872 | tf_op jit(solution)/shard_map/ppermute | solution.py:221
  67.8 34.4 %collective-permute-start.10 = (bf16[256,1024]{1,0:T(8,128)(2,1)}, bf16[256,1024]{1,0:T(8,128)(2,1)S(1)}, u32[]{:S(2)}, u32[]{:S(2)}) collective-permute-start(bf16[256,1024]{1,0:T(8,128)(2,1)} %get-tuple-element.49), channel_id=1, source_target_pairs={{2,0},{3,1},{0,2},{1,3},{6,4},{7,5},{4,6},{5,7},{10,8},{11,9},{8,1... | collective-permute-start | bytes 1572872 | tf_op jit(solution)/shard_map/ppermute | solution.py:221
  77.3 19.2 %collective-permute-start.12 = (bf16[128,1024]{1,0:T(8,128)(2,1)S(1)}, bf16[128,1024]{1,0:T(8,128)(2,1)S(1)}, u32[]{:S(2)}, u32[]{:S(2)}) collective-permute-start(bf16[128,1024]{1,0:T(8,128)(2,1)S(1)} %collective-permute-done.3.far_a.refs_7_), channel_id=1, source_target_pairs={{0,4},{4,0},{1,5},{5,1},{2,6},{6,2},{3,7},{7,3},{8,12},{12,8},{9,1... | collective-permute-start | bytes 786440 | tf_op jit(solution)/shard_map/ppermute | solution.py:236
  77.6 24.6 %collective-permute-start.13 = (bf16[128,1024]{1,0:T(8,128)(2,1)S(1)}, bf16[128,1024]{1,0:T(8,128)(2,1)S(1)}, u32[]{:S(2)}, u32[]{:S(2)}) collective-permute-start(bf16[128,1024]{1,0:T(8,128)(2,1)S(1)} %copy-done.15), channel_id=1, source_target_pairs={{0,4},{4,0},{1,5},{5,1},{2,6},{6,2},{3,7},{7,3},{8,12},{12,8},{9,1... | collective-permute-start | bytes 786440 | tf_op jit(solution)/shard_map/ppermute | solution.py:237
  112.9 3.0 %collective-permute-start.21 = (bf16[8,64,1024]{2,1,0:T(8,128)(2,1)}, bf16[8,64,1024]{2,1,0:T(8,128)(2,1)S(1)}, u32[]{:S(2)}, u32[]{:S(2)}) collective-permute-start(bf16[8,64,1024]{2,1,0:T(8,128)(2,1)} %get-tuple-element.76), channel_id=1, source_target_pairs={{0,8},{8,0},{1,9},{9,1},{2,10},{10,2},{3,11},{11,3},{4,12},{12,4},... | collective-permute-start | bytes 3145736 | tf_op jit(solution)/shard_map/ppermute | solution.py:260
  117.6 24.0 %copy-start.4 = (f32[1,64,1024]{2,1,0:T(8,128)S(1)}, f32[1,64,1024]{2,1,0:T(8,128)}, u32[]{:S(2)}) copy-start(f32[1,64,1024]{2,1,0:T(8,128)} %param.11) | copy-start | bytes 786436
  143.6 20.9 %all-to-all-start.1 = ((bf16[8,64,1024]{2,1,0:T(8,128)(2,1)}), bf16[8,64,1024]{2,1,0:T(8,128)(2,1)S(1)}, u32[]{:S(2)}, u32[]{:S(2)}) async-start(bf16[8,64,1024]{2,1,0:T(8,128)(2,1)} %broadcast_in_dim.36), calls=%async_computation.1 | async-start | bytes 2097152 | tf_op jit(solution)/shard_map/all_to_all | solution.py:267
  147.2 25.1 %collective-permute-start.18 = (bf16[2,256,1024]{2,1,0:T(8,128)(2,1)}, bf16[2,256,1024]{2,1,0:T(8,128)(2,1)S(1)}, u32[]{:S(2)}, u32[]{:S(2)}) collective-permute-start(bf16[2,256,1024]{2,1,0:T(8,128)(2,1)} %get-tuple-element.63), channel_id=1, source_target_pairs={{0,1},{1,2},{2,3},{3,0},{4,5},{5,6},{6,7},{7,4},{8,9},{9,10},{10,1... | collective-permute-start | bytes 3145736 | tf_op jit(solution)/shard_map/ppermute | solution.py:253
  147.3 25.0 %collective-permute-start.19 = (bf16[2,256,1024]{2,1,0:T(8,128)(2,1)}, bf16[2,256,1024]{2,1,0:T(8,128)(2,1)S(1)}, u32[]{:S(2)}, u32[]{:S(2)}) collective-permute-start(bf16[2,256,1024]{2,1,0:T(8,128)(2,1)} %get-tuple-element.64), channel_id=1, source_target_pairs={{0,3},{1,0},{2,1},{3,2},{4,7},{5,4},{6,5},{7,6},{8,11},{9,8},{10,9... | collective-permute-start | bytes 3145736 | tf_op jit(solution)/shard_map/ppermute | solution.py:254
  149.9 44.7 %collective-permute-start.20 = (bf16[2,256,1024]{2,1,0:T(8,128)(2,1)}, bf16[2,256,1024]{2,1,0:T(8,128)(2,1)}, u32[]{:S(2)}, u32[]{:S(2)}) collective-permute-start(bf16[2,256,1024]{2,1,0:T(8,128)(2,1)} %get-tuple-element.65), channel_id=1, source_target_pairs={{0,2},{1,3},{2,0},{3,1},{4,6},{5,7},{6,4},{7,5},{8,10},{9,11},{10,... | collective-permute-start | bytes 3145736 | tf_op jit(solution)/shard_map/ppermute | solution.py:255
  164.5 34.2 %collective-permute-start.22 = (bf16[8,64,1024]{2,1,0:T(8,128)(2,1)S(1)}, bf16[8,64,1024]{2,1,0:T(8,128)(2,1)}, u32[]{:S(2)}, u32[]{:S(2)}) collective-permute-start(bf16[8,64,1024]{2,1,0:T(8,128)(2,1)S(1)} %all-to-all-done.1), channel_id=1, source_target_pairs={{0,8},{8,0},{1,9},{9,1},{2,10},{10,2},{3,11},{11,3},{4,12},{12,4},... | collective-permute-start | bytes 3145736 | tf_op jit(solution)/shard_map/ppermute | solution.py:268
  172.2 22.4 %copy-start.2 = (bf16[2,256,1024]{2,1,0:T(8,128)(2,1)}, bf16[2,256,1024]{2,1,0:T(8,128)(2,1)S(1)}, u32[]{:S(2)}) copy-start(bf16[2,256,1024]{2,1,0:T(8,128)(2,1)S(1)} %collective-permute-done.18.refs_1_) | copy-start | bytes 3145732
  172.2 22.4 %copy-start.3 = (bf16[2,256,1024]{2,1,0:T(8,128)(2,1)}, bf16[2,256,1024]{2,1,0:T(8,128)(2,1)S(1)}, u32[]{:S(2)}) copy-start(bf16[2,256,1024]{2,1,0:T(8,128)(2,1)S(1)} %collective-permute-done.19.refs_2_) | copy-start | bytes 3145732
  (10 other events, 54.2 us)

commit v2 on v1

--- a/solution.py
+++ b/solution.py
@@ -12,6 +12,7 @@
 BLK = 1024
 KV = 1024
 OWN = 64
+GRANT = 20 * 2**20
 SHARD = ("zl", "y")
 CHIPS = ("zh", "x")
 Z = ("zh", "zl")
@@ -71,6 +72,7 @@
             bytes_accessed=(4 + 4 * len(rest) + n) * 2**20,
             transcendentals=0,
         ),
+        compiler_params=pltpu.CompilerParams(vmem_limit_bytes=GRANT),
     )(*feats, *keys, *rest)
 
 
@@ -115,6 +117,7 @@
         cost_estimate=pl.CostEstimate(
             flops=2 * sum(key_rows) * BLK * KV, bytes_accessed=14 * 2**20, transcendentals=BLK * KV
         ),
+        compiler_params=pltpu.CompilerParams(vmem_limit_bytes=GRANT),
         name="late",
     )(core, *feats, *keys, base)
 
@@ -156,6 +159,7 @@
         cost_estimate=pl.CostEstimate(
             flops=2 * 4 * TOK * 2 * BLK * KV, bytes_accessed=10 * 2**20, transcendentals=0
         ),
+        compiler_params=pltpu.CompilerParams(vmem_limit_bytes=GRANT),
         name="back",
     )(core, *blocks, weight, got, got_other)
 
@@ -192,6 +196,7 @@
             pltpu.SemaphoreType.DMA((n, 2)),
         ],
         cost_estimate=pl.CostEstimate(flops=0, bytes_accessed=8 * 2**20, transcendentals=0),
+        compiler_params=pltpu.CompilerParams(vmem_limit_bytes=GRANT),
         name="place",
     )(at, *pieces)
 
@@ -211,7 +216,7 @@
     k01 = lax.ppermute(key_grads, "y", shift_y(-1))
     half_weight = lax.dynamic_slice_in_dim(key_weight, core * (BLK // 2), BLK // 2, axis=0)
     got = lax.ppermute(half_weight, Z, z_perm())
-    order = [(0, 0), (1, 0), (0, 1), (0, 3), (1, 2), (1, 1), (1, 3), (0, 2)]
+    order = [(0, 0), (1, 0), (1, 1), (1, 3), (1, 2), (0, 1), (0, 3), (0, 2)]
     pieces = {k: columns(*k) for k in order}
     flat = fence((k10, k03, k01) + tuple(pieces.values()))
     k10, k03, k01 = flat[:3]
@@ -230,23 +235,23 @@
 
     base = early_call(first_kernel, [feats[0, 0]], [key_grads], [momentum[0], worker_error[0]])
 
-    flat = fence((far_a, far_b, k13, k11, got) + tuple(pieces[k] for k in order[5:]))
-    far_a, far_b, k13, k11, got = flat[:5]
-    pieces.update(zip(order[5:], flat[5:]))
+    flat = fence((far_a, far_b, got) + tuple(pieces[k] for k in order[5:]))
+    far_a, far_b, got = flat[:3]
+    pieces.update(zip(order[5:], flat[3:]))
     zfar_a = lax.ppermute(far_a, "zl", SWAP)
     zfar_b = lax.ppermute(far_b, "zl", SWAP)
     for key in order[5:]:
         feats[key] = send(key)
 
     got_other = lax.ppermute(got, "core", SWAP)
-    early = [(1, 0), (0, 1), (0, 3)]
-    early_keys = [k10, k01, k03]
+    early = [(1, 0), (1, 1), (1, 3)]
+    early_keys = [k10, k11, k13]
     base = early_call(
         lambda *refs: early_kernel(len(early), *refs), [feats[k] for k in early], early_keys, [base]
     )
     backs = back_call(core_arg, (key_grads, k01, k03, far_a, far_b), key_weight, got, got_other)
 
-    late = [(1, 1), (1, 3), (0, 2), (1, 2)]
+    late = [(0, 1), (0, 3), (0, 2), (1, 2)]
     flat = fence(tuple(feats[k] for k in late) + (zfar_a, zfar_b, base) + tuple(backs))
     late_feats, (zfar_a, zfar_b, base), backs = flat[:4], flat[4:7], flat[7:]
     back_own, back_1, back_3, back_2 = backs
@@ -254,7 +259,7 @@
     home_3 = lax.ppermute(back_3, "y", shift_y(-1))
     home_2 = lax.ppermute(back_2, "y", shift_y(2))
     new_worker, mine, other = late_call(
-        core_arg, list(late_feats), [k11, k13, far_a, far_b, zfar_a, zfar_b], base
+        core_arg, list(late_feats), [k01, k03, far_a, far_b, zfar_a, zfar_b], base
     )
 
     met = lax.ppermute(other, "core", SWAP)

time: 204 us -> 200 us (0.980)
  waiting for transfers between devices: 89.5 us -> 104 us
  Pallas kernels: 36.8 us -> 23.2 us
  local copies, waits for them, and re-layouts: 8.97 us -> 5.46 us
  starting transfers between devices: 35.2 us -> 38.6 us
    ppermute x7, waiting for transfers between devices: 13.9 us -> 37.7 us  [send(): return lax.ppermute(pieces[key], SHARD, shard_perm(*key))]
    ppermute x1, waiting for transfers between devices: 6.04 us -> 28.9 us  [per_device(): home_1 = lax.ppermute(back_1, 'y', shift_y(1))]
    ppermute x1, waiting for transfers between devices: 22.4 us -> 0.01 us  [per_device(): home_2 = lax.ppermute(back_2, 'y', shift_y(2))]
    ppermute x1, waiting for transfers between devices: 13.2 us -> 2.24 us  [per_device(): far_a = lax.ppermute(k03[:TOK // 2], 'y', shift_y(1))]
    pallas_call x2, Pallas kernels: 13.7 us -> 4.31 us  [early_call(): pl.pallas_call(kernel, out_shape=jax.ShapeDtypeStruct((BLK, KV), jnp.floa...]
    ppermute x1, waiting for transfers between devices: 8.03 us -> 0.01 us  [per_device(): zfar_a = lax.ppermute(far_a, 'zl', SWAP)]
    ppermute x1, waiting for transfers between devices: 0.01 us -> 7.52 us  [per_device(): k13 = lax.ppermute(k10, 'y', shift_y(1))]
    ppermute x1, waiting for transfers between devices: 1.35 us -> 7.04 us  [per_device(): k10 = lax.ppermute(key_grads, 'zl', SWAP)]
  transfers between devices with their start and end apart: 24 -> 24, of which waited for: 12 -> 13; matrix products, arithmetic and copies ran while one was open for 3% -> 2% of each run, Pallas kernels for 14% -> 8%
where the time goes in v2:
time: 200 us; the launch traced here: 199 us
  waiting for transfers between devices  104 us (52%)
  starting transfers between devices  38.6 us (19%)
  Pallas kernels  23.2 us (12%)
  blocking collectives  22.1 us (11%)
  local copies, waits for them, and re-layouts  5.46 us (3%)
  other arithmetic  4.85 us (2%)
    ppermute x7, waiting for transfers between devices, send(): return lax.ppermute(pieces[key], SHARD, shard_perm(*key))  37.7 us
    ppermute x1, waiting for transfers between devices, per_device(): home_1 = lax.ppermute(back_1, 'y', shift_y(1))  28.9 us
    all_to_all x1, blocking collectives, per_device(): parts = lax.all_to_all(pair, CHIPS, 0, 0)  22.1 us
    all_to_all x1, waiting for transfers between devices, per_device(): lax.all_to_all(jnp.broadcast_to(block[None], (8, OWN, KV)), CHIPS, 0, 0)  14.6 us
    ppermute x7, starting transfers between devices, send(): return lax.ppermute(pieces[key], SHARD, shard_perm(*key))  8.95 us
    pallas_call x1, Pallas kernels, back_call(): pl.pallas_call(back_kernel, out_shape=(out,) * 4, grid_spec=pltpu.Prefetc...  8.45 us
    ppermute x1, waiting for transfers between devices, per_device(): k13 = lax.ppermute(k10, 'y', shift_y(1))  7.52 us
    ppermute x1, waiting for transfers between devices, per_device(): k10 = lax.ppermute(key_grads, 'zl', SWAP)  7.04 us
  transfers between devices with their start and end apart: 24, of which 13 were waited for; matrix products, arithmetic and copies ran while one was open for 2% of the time, Pallas kernels for 8%

profile of v2, /device:TPU:1, one launch (start us, length us, event | category | flops | bytes accessed | tf_op | source)
XLA Modules:
  0.0 199.3 jit_solution(15691381149259507464)
XLA Ops:
  0.6 1.4 constant_dynamic-slice_fusion
  2.0 4.7 %collective-permute-start.5 = (bf16[512,1024]{1,0:T(8,128)(2,1)S(1)}, bf16[512,1024]{1,0:T(8,128)(2,1)}, u32[]{:S(2)}, u32[]{:S(2)}) collective-permute-start(bf16[512,1024]{1,0:T(8,128)(2,1)S(1)} %constant_dynamic-slice_fusion), channel_id=1, source_target_pairs={{0,68},{4,64},{64,4},{68,0},{1,69},{5,65},{65,5},{69,1},{2,70},{6,... | collective-permute-start | bytes 3145736 | tf_op jit(solution)/shard_map/ppermute | solution.py:218
  8.0 1.5 collective-permute-start.2
  9.5 2.8 %constant_dynamic-slice_fusion.1 = (bf16[256,1024]{1,0:T(8,128)(2,1)S(1)}, bf16[256,1024]{1,0:T(8,128)(2,1)S(1)}, bf16[256,1024]{1,0:T(8,128)(2,1)S(1)}, bf16[25...) fusion(bf16[256,8192]{1,0:T(8,128)(2,1)} %param.6, ...), kind=kLoop, calls=%fused_computation.10 | loop fusion | bytes 8388640 | tf_op jit(solution)/shard_map/dynamic_slice | solution.py:212
  12.3 7.0 %collective-permute-done.refs_3_ = bf16[256,1024]{1,0:T(8,128)(2,1)S(1)} collective-permute-done((bf16[256,1024]{1,0:T(8,128)(2,1)S(1)}, bf16[256,1024]{1,0:T(8,128)(2,1)S(1)}, u32[]{:S(2)}, u32[]{:S(2)}) %collective-permute-start) | collective-permute-done | bytes 524320 | tf_op jit(solution)/shard_map/ppermute | solution.py:214
  21.7 1.8 collective-permute-start.4
  24.6 1.4 collective-permute-start.13
  26.0 2.2 %collective-permute-done.3.far_a.refs_7_ = bf16[128,1024]{1,0:T(8,128)(2,1)S(1)} collective-permute-done((bf16[128,1024]{1,0:T(8,128)(2,1)S(1)}, bf16[128,1024]{1,0:T(8,128)(2,1)S(1)}, u32[]{:S(2)}, u32[]{:S(2)}) %collective-permute-start.3) | collective-permute-done | bytes 262176 | tf_op jit(solution)/shard_map/ppermute | solution.py:229
  28.2 1.4 collective-permute-done.5.got
  29.6 3.6 %collective-permute-start.17 = (bf16[512,1024]{1,0:T(8,128)(2,1)}, bf16[512,1024]{1,0:T(8,128)(2,1)S(1)}, u32[]{:S(2)}, u32[]{:S(2)}) collective-permute-start(bf16[512,1024]{1,0:T(8,128)(2,1)} %collective-permute-done.5.got), channel_id=1, source_target_pairs={{0,8},{8,0},{1,9},{9,1},{2,10},{10,2},{3,11},{11,3},{4,12},{12,4},... | collective-permute-start | bytes 3145736 | tf_op jit(solution)/shard_map/ppermute | solution.py:246
  33.2 2.2 %collective-permute-start.14 = (bf16[256,1024]{1,0:T(8,128)(2,1)S(1)}, bf16[256,1024]{1,0:T(8,128)(2,1)S(1)}, u32[]{:S(2)}, u32[]{:S(2)}) collective-permute-start(bf16[256,1024]{1,0:T(8,128)(2,1)S(1)} %get-tuple-element.52), channel_id=1, source_target_pairs={{7,0},{4,1},{5,2},{6,3},{3,4},{0,5},{1,6},{2,7},{15,8},{12,9},{13,... | collective-permute-start | bytes 1572872 | tf_op jit(solution)/shard_map/ppermute | solution.py:226
  35.4 1.7 collective-permute-start.15
  37.1 20.6 %collective-permute-done.12.refs_0_ = bf16[256,1024]{1,0:T(8,128)(2,1)S(1)} collective-permute-done((bf16[256,1024]{1,0:T(8,128)(2,1)S(1)}, bf16[256,1024]{1,0:T(8,128)(2,1)S(1)}, u32[]{:S(2)}, u32[]{:S(2)}) %collective-permute-start.12) | collective-permute-done | bytes 524320 | tf_op jit(solution)/shard_map/ppermute | solution.py:226
  57.7 2.1 %collective-permute-start.9 = (bf16[256,1024]{1,0:T(8,128)(2,1)S(1)}, bf16[256,1024]{1,0:T(8,128)(2,1)S(1)}, u32[]{:S(2)}, u32[]{:S(2)}) collective-permute-start(bf16[256,1024]{1,0:T(8,128)(2,1)S(1)} %get-tuple-element.47), channel_id=1, source_target_pairs={{6,0},{7,1},{4,2},{5,3},{2,4},{3,5},{0,6},{1,7},{14,8},{15,9},{12,... | collective-permute-start | bytes 1572872 | tf_op jit(solution)/shard_map/ppermute | solution.py:226
  59.7 1.6 shard_map.93.refs_6_
  63.6 7.5 %collective-permute-done.16.refs_5_ = bf16[256,1024]{1,0:T(8,128)(2,1)S(1)} collective-permute-done((bf16[256,1024]{1,0:T(8,128)(2,1)S(1)}, bf16[256,1024]{1,0:T(8,128)(2,1)S(1)}, u32[]{:S(2)}, u32[]{:S(2)}) %collective-permute-start.16) | collective-permute-done | bytes 524320 | tf_op jit(solution)/shard_map/ppermute | solution.py:231
  71.1 2.7 %shard_map.94.refs_11_ = f32[1024,1024]{1,0:T(8,128)S(1)} custom-call(bf16[256,1024]{1,0:T(8,128)(2,1)S(1)} %collective-permute-done.12.refs_0_, bf16[256,1024]{1,0:T(8,128)(2,1)S(1)} %collective-permute-done.13.refs_1_, bf16[256,1024]{1,0:T(8,128)(2,1)S(1)} %collective-permute-done.14.refs_2_, bf16[256,1024]{1,0:T(8,128)(2,1)S(1)} %collective-permute-done.refs_3_, ...), custom_call_target="tpu_custom_call" | custom-call | flops 1610612736 | bytes 11534336 | tf_op jit(solution)/shard_map/pallas_call | solution.py:64
  73.8 5.5 %collective-permute-done.9.refs_4_ = bf16[256,1024]{1,0:T(8,128)(2,1)S(1)} collective-permute-done((bf16[256,1024]{1,0:T(8,128)(2,1)S(1)}, bf16[256,1024]{1,0:T(8,128)(2,1)S(1)}, u32[]{:S(2)}, u32[]{:S(2)}) %collective-permute-start.9) | collective-permute-done | bytes 524320 | tf_op jit(solution)/shard_map/ppermute | solution.py:226
  79.3 1.4 collective-permute-start.10
  80.8 8.5 %back.1 = (bf16[2,256,1024]{2,1,0:T(8,128)(2,1)S(1)}, bf16[2,256,1024]{2,1,0:T(8,128)(2,1)}, bf16[2,256,1024]{2,1,0:T(8,128)(2,1)S(1)}, bf16[2,256,1024]{2,1,0:T(8,128)(2,1)S(1)}) custom-call(s32[1]{0:T(128)} %bitcast.14.core_ref.refs_0_, bf16[256,1024]{1,0:T(8,128)(2,1)S(1)} %copy-done.3, bf16[256,1024]{1,0:T(8,128)(2,1)S(1)} %collective-permute-done.2.left.refs_5_, ...), custom_call_target="tpu_custom_call" | custom-call | flops 4294967296 | bytes 10485760 | tf_op jit(solution)/shard_map/back/pallas_call | solution.py:149
  90.5 3.1 %collective-permute-done.7.refs_2_ = bf16[256,1024]{1,0:T(8,128)(2,1)S(1)} collective-permute-done((bf16[256,1024]{1,0:T(8,128)(2,1)S(1)}, bf16[256,1024]{1,0:T(8,128)(2,1)S(1)}, u32[]{:S(2)}, u32[]{:S(2)}) %collective-permute-start.7) | collective-permute-done | bytes 524320 | tf_op jit(solution)/shard_map/ppermute | solution.py:226
  93.6 8.5 %collective-permute-done.8.refs_3_ = bf16[256,1024]{1,0:T(8,128)(2,1)S(1)} collective-permute-done((bf16[256,1024]{1,0:T(8,128)(2,1)S(1)}, bf16[256,1024]{1,0:T(8,128)(2,1)S(1)}, u32[]{:S(2)}, u32[]{:S(2)}) %collective-permute-start.8) | collective-permute-done | bytes 524320 | tf_op jit(solution)/shard_map/ppermute | solution.py:226
  102.1 6.6 %late.1 = (f32[1024,1024]{1,0:T(8,128)}, bf16[8,64,1024]{2,1,0:T(8,128)(2,1)S(1)}, bf16[8,64,1024]{2,1,0:T(8,128)(2,1)S(1)}) custom-call(s32[1]{0:T(128)} %bitcast.14.core_ref.refs_0_, bf16[256,1024]{1,0:T(8,128)(2,1)S(1)} %collective-permute-done.6.refs_1_, bf16[256,1024]{1,0:T(8,128)(2,1)S(1)} %collective-permute-done.7.refs_2_, ...), custom_call_target="tpu_custom_call" | custom-call | flops 2147483648 | bytes 14680064 | tf_op jit(solution)/shard_map/late/pallas_call | solution.py:108
  108.7 4.8 %collective-permute-start.21 = (bf16[8,64,1024]{2,1,0:T(8,128)(2,1)S(1)}, bf16[8,64,1024]{2,1,0:T(8,128)(2,1)S(1)}, u32[]{:S(2)}, u32[]{:S(2)}) collective-permute-start(bf16[8,64,1024]{2,1,0:T(8,128)(2,1)S(1)} %get-tuple-element.72), channel_id=1, source_target_pairs={{0,8},{8,0},{1,9},{9,1},{2,10},{10,2},{3,11},{11,3},{4,12},{12,4},... | collective-permute-start | bytes 3145736 | tf_op jit(solution)/shard_map/ppermute | solution.py:265
  113.6 2.3 %collective-permute-done.21 = bf16[8,64,1024]{2,1,0:T(8,128)(2,1)S(1)} collective-permute-done((bf16[8,64,1024]{2,1,0:T(8,128)(2,1)S(1)}, bf16[8,64,1024]{2,1,0:T(8,128)(2,1)S(1)}, u32[]{:S(2)}, u32[]{:S(2)}) %collective-permute-start.21) | collective-permute-done | bytes 1048608 | tf_op jit(solution)/shard_map/ppermute | solution.py:265
  116.3 22.1 %all_to_all.10 = bf16[8,64,1024]{2,1,0:T(8,128)(2,1)S(1)} all-to-all(bf16[8,64,1024]{2,1,0:T(8,128)(2,1)S(1)} %add_convert_fusion), channel_id=1, replica_groups=mesh['zh'=2,'x'=4,'core'=2,'zl'=2,'y'=4] {'zh','x'}, dimensions={0} | all-to-all | bytes 2097152 | tf_op jit(solution)/shard_map/all_to_all | solution.py:267
  140.6 4.2 %all-to-all-start.1 = ((bf16[8,64,1024]{2,1,0:T(8,128)(2,1)}), bf16[8,64,1024]{2,1,0:T(8,128)(2,1)}, u32[]{:S(2)}, u32[]{:S(2)}) async-start(bf16[8,64,1024]{2,1,0:T(8,128)(2,1)} %broadcast_in_dim.36), calls=%async_computation.1 | async-start | bytes 2097152 | tf_op jit(solution)/shard_map/all_to_all | solution.py:272
  145.0 2.7 %collective-permute-start.19 = (bf16[2,256,1024]{2,1,0:T(8,128)(2,1)}, bf16[2,256,1024]{2,1,0:T(8,128)(2,1)S(1)}, u32[]{:S(2)}, u32[]{:S(2)}) collective-permute-start(bf16[2,256,1024]{2,1,0:T(8,128)(2,1)} %copy-done.5), channel_id=1, source_target_pairs={{0,3},{1,0},{2,1},{3,2},{4,7},{5,4},{6,5},{7,6},{8,11},{9,8},{10,9... | collective-permute-start | bytes 3145736 | tf_op jit(solution)/shard_map/ppermute | solution.py:259
  147.6 14.6 %all-to-all-done.1 = bf16[8,64,1024]{2,1,0:T(8,128)(2,1)} async-done(((bf16[8,64,1024]{2,1,0:T(8,128)(2,1)}), bf16[8,64,1024]{2,1,0:T(8,128)(2,1)}, u32[]{:S(2)}, u32[]{:S(2)}) %all-to-all-start.1) | async-done | bytes 1048608 | tf_op jit(solution)/shard_map/all_to_all | solution.py:272
  163.4 28.9 %collective-permute-done.18.refs_1_ = bf16[2,256,1024]{2,1,0:T(8,128)(2,1)S(1)} collective-permute-done((bf16[2,256,1024]{2,1,0:T(8,128)(2,1)}, bf16[2,256,1024]{2,1,0:T(8,128)(2,1)S(1)}, u32[]{:S(2)}, u32[]{:S(2)}) %collective-permute-start.18) | collective-permute-done | bytes 1048608 | tf_op jit(solution)/shard_map/ppermute | solution.py:258
  192.3 3.8 %place.1 = bf16[256,8192]{1,0:T(8,128)(2,1)} custom-call(s32[4,2]{1,0:T(4,128)S(1)} %pad_add_fusion.at_ref, bf16[2,256,1024]{2,1,0:T(8,128)(2,1)S(1)} %get-tuple-element.60.refs_0_, bf16[2,256,1024]{2,1,0:T(8,128)(2,1)S(1)} %collective-permute-done.18.refs_1_, bf16[2,256,1024]{2,1,0:T(8,128)(2,1)S(1)} %collective-permute-done.19.refs_2_, ...), custom_call_target="tpu_custom_call" | custom-call | bytes 8388608 | tf_op jit(solution)/shard_map/place/pallas_call | solution.py:188
  196.2 3.1 %bitcast_select_fusion = bf16[1024,1024]{1,0:T(8,128)(2,1)} fusion(pred[1024]{0:T(1024)(128)(4,1)S(1)} %iota.12, bf16[8,64,1024]{2,1,0:T(8,128)(2,1)} %collective-permute-done.22, bf16[8,64,1024]{2,1,0:T(8,128)(2,1)} %all-to-all-done.1), kind=kLoop, calls=%fused_computation | loop fusion | flops 1048576 | bytes 4195328 | tf_op jit(solution)/shard_map/jit(_where)/select_n | solution.py:275
  (53 shorter events, 12.2 us)
Async XLA Ops:
  0.6 6.0 %copy-start.3 = (bf16[256,1024]{1,0:T(8,128)(2,1)S(1)}, bf16[256,1024]{1,0:T(8,128)(2,1)}, u32[]{:S(2)}) copy-start(bf16[256,1024]{1,0:T(8,128)(2,1)} %own.1) | copy-start | bytes 1572868
  2.0 27.6 %collective-permute-start.5 = (bf16[512,1024]{1,0:T(8,128)(2,1)S(1)}, bf16[512,1024]{1,0:T(8,128)(2,1)}, u32[]{:S(2)}, u32[]{:S(2)}) collective-permute-start(bf16[512,1024]{1,0:T(8,128)(2,1)S(1)} %constant_dynamic-slice_fusion), channel_id=1, source_target_pairs={{0,68},{4,64},{64,4},{68,0},{1,69},{5,65},{65,5},{69,1},{2,70},{6,... | collective-permute-start | bytes 3145736 | tf_op jit(solution)/shard_map/ppermute | solution.py:218
  6.7 12.6 %collective-permute-start = (bf16[256,1024]{1,0:T(8,128)(2,1)S(1)}, bf16[256,1024]{1,0:T(8,128)(2,1)S(1)}, u32[]{:S(2)}, u32[]{:S(2)}) collective-permute-start(bf16[256,1024]{1,0:T(8,128)(2,1)S(1)} %copy-done.3), channel_id=1, source_target_pairs={{0,4},{4,0},{1,5},{5,1},{2,6},{6,2},{3,7},{7,3},{8,12},{12,8},{9,1... | collective-permute-start | bytes 1572872 | tf_op jit(solution)/shard_map/ppermute | solution.py:214
  6.7 14.0 %collective-permute-start.1 = (bf16[256,1024]{1,0:T(8,128)(2,1)S(1)}, bf16[256,1024]{1,0:T(8,128)(2,1)S(1)}, u32[]{:S(2)}, u32[]{:S(2)}) collective-permute-start(bf16[256,1024]{1,0:T(8,128)(2,1)S(1)} %copy-done.3), channel_id=1, source_target_pairs={{0,1},{1,2},{2,3},{3,0},{4,5},{5,6},{6,7},{7,4},{8,9},{9,10},{10,1... | collective-permute-start | bytes 1572872 | tf_op jit(solution)/shard_map/ppermute | solution.py:215
  8.0 12.7 %collective-permute-start.2 = (bf16[256,1024]{1,0:T(8,128)(2,1)S(1)}, bf16[256,1024]{1,0:T(8,128)(2,1)S(1)}, u32[]{:S(2)}, u32[]{:S(2)}) collective-permute-start(bf16[256,1024]{1,0:T(8,128)(2,1)S(1)} %copy-done.3), channel_id=1, source_target_pairs={{0,3},{1,0},{2,1},{3,2},{4,7},{5,4},{6,5},{7,6},{8,11},{9,8},{10,9... | collective-permute-start | bytes 1572872 | tf_op jit(solution)/shard_map/ppermute | solution.py:216
  9.5 50.3 %copy-start = (f32[1,1024,1024]{2,1,0:T(8,128)S(1)}, f32[1,1024,1024]{2,1,0:T(8,128)}, u32[]{:S(2)}) copy-start(f32[1,1024,1024]{2,1,0:T(8,128)} %param.9) | copy-start | bytes 12582916
  9.5 50.3 %copy-start.1 = (f32[1,1024,1024]{2,1,0:T(8,128)S(1)}, f32[1,1024,1024]{2,1,0:T(8,128)}, u32[]{:S(2)}) copy-start(f32[1,1024,1024]{2,1,0:T(8,128)} %param.10) | copy-start | bytes 12582916
  20.7 7.6 %collective-permute-start.3 = (bf16[128,1024]{1,0:T(8,128)(2,1)S(1)}, bf16[128,1024]{1,0:T(8,128)(2,1)S(1)}, u32[]{:S(2)}, u32[]{:S(2)}) collective-permute-start(bf16[128,1024]{1,0:T(8,128)(2,1)S(1)} %slice.6), channel_id=1, source_target_pairs={{0,1},{1,2},{2,3},{3,0},{4,5},{5,6},{6,7},{7,4},{8,9},{9,10},{10,1... | collective-permute-start | bytes 786440 | tf_op jit(solution)/shard_map/ppermute | solution.py:229
  21.7 6.5 %collective-permute-start.4 = (bf16[128,1024]{1,0:T(8,128)(2,1)S(1)}, bf16[128,1024]{1,0:T(8,128)(2,1)S(1)}, u32[]{:S(2)}, u32[]{:S(2)}) collective-permute-start(bf16[128,1024]{1,0:T(8,128)(2,1)S(1)} %slice.7), channel_id=1, source_target_pairs={{0,3},{1,0},{2,1},{3,2},{4,7},{5,4},{6,5},{7,6},{8,11},{9,8},{10,9... | collective-permute-start | bytes 786440 | tf_op jit(solution)/shard_map/ppermute | solution.py:230
  23.5 34.2 %collective-permute-start.12 = (bf16[256,1024]{1,0:T(8,128)(2,1)S(1)}, bf16[256,1024]{1,0:T(8,128)(2,1)S(1)}, u32[]{:S(2)}, u32[]{:S(2)}) collective-permute-start(bf16[256,1024]{1,0:T(8,128)(2,1)S(1)} %get-tuple-element.50), channel_id=1, source_target_pairs={{4,0},{5,1},{6,2},{7,3},{0,4},{1,5},{2,6},{3,7},{12,8},{13,9},{14,... | collective-permute-start | bytes 1572872 | tf_op jit(solution)/shard_map/ppermute | solution.py:226
  24.6 33.1 %collective-permute-start.13 = (bf16[256,1024]{1,0:T(8,128)(2,1)S(1)}, bf16[256,1024]{1,0:T(8,128)(2,1)S(1)}, u32[]{:S(2)}, u32[]{:S(2)}) collective-permute-start(bf16[256,1024]{1,0:T(8,128)(2,1)S(1)} %get-tuple-element.51), channel_id=1, source_target_pairs={{5,0},{6,1},{7,2},{4,3},{1,4},{2,5},{3,6},{0,7},{13,8},{14,9},{15,... | collective-permute-start | bytes 1572872 | tf_op jit(solution)/shard_map/ppermute | solution.py:226
  29.6 51.1 %collective-permute-start.17 = (bf16[512,1024]{1,0:T(8,128)(2,1)}, bf16[512,1024]{1,0:T(8,128)(2,1)S(1)}, u32[]{:S(2)}, u32[]{:S(2)}) collective-permute-start(bf16[512,1024]{1,0:T(8,128)(2,1)} %collective-permute-done.5.got), channel_id=1, source_target_pairs={{0,8},{8,0},{1,9},{9,1},{2,10},{10,2},{3,11},{11,3},{4,12},{12,4},... | collective-permute-start | bytes 3145736 | tf_op jit(solution)/shard_map/ppermute | solution.py:246
  33.2 28.2 %collective-permute-start.14 = (bf16[256,1024]{1,0:T(8,128)(2,1)S(1)}, bf16[256,1024]{1,0:T(8,128)(2,1)S(1)}, u32[]{:S(2)}, u32[]{:S(2)}) collective-permute-start(bf16[256,1024]{1,0:T(8,128)(2,1)S(1)} %get-tuple-element.52), channel_id=1, source_target_pairs={{7,0},{4,1},{5,2},{6,3},{3,4},{0,5},{1,6},{2,7},{15,8},{12,9},{13,... | collective-permute-start | bytes 1572872 | tf_op jit(solution)/shard_map/ppermute | solution.py:226
  35.4 27.2 %collective-permute-start.15 = (bf16[256,1024]{1,0:T(8,128)(2,1)S(1)}, bf16[256,1024]{1,0:T(8,128)(2,1)S(1)}, u32[]{:S(2)}, u32[]{:S(2)}) collective-permute-start(bf16[256,1024]{1,0:T(8,128)(2,1)S(1)} %collective-permute-done.refs_3_), channel_id=1, source_target_pairs={{0,3},{1,0},{2,1},{3,2},{4,7},{5,4},{6,5},{7,6},{8,11},{9,8},{10,9... | collective-permute-start | bytes 1572872 | tf_op jit(solution)/shard_map/ppermute | solution.py:232
  57.7 13.5 %collective-permute-start.16 = (bf16[256,1024]{1,0:T(8,128)(2,1)S(1)}, bf16[256,1024]{1,0:T(8,128)(2,1)S(1)}, u32[]{:S(2)}, u32[]{:S(2)}) collective-permute-start(bf16[256,1024]{1,0:T(8,128)(2,1)S(1)} %collective-permute-done.refs_3_), channel_id=1, source_target_pairs={{0,1},{1,2},{2,3},{3,0},{4,5},{5,6},{6,7},{7,4},{8,9},{9,10},{10,1... | collective-permute-start | bytes 1572872 | tf_op jit(solution)/shard_map/ppermute | solution.py:231
  57.7 21.6 %collective-permute-start.9 = (bf16[256,1024]{1,0:T(8,128)(2,1)S(1)}, bf16[256,1024]{1,0:T(8,128)(2,1)S(1)}, u32[]{:S(2)}, u32[]{:S(2)}) collective-permute-start(bf16[256,1024]{1,0:T(8,128)(2,1)S(1)} %get-tuple-element.47), channel_id=1, source_target_pairs={{6,0},{7,1},{4,2},{5,3},{2,4},{3,5},{0,6},{1,7},{14,8},{15,9},{12,... | collective-permute-start | bytes 1572872 | tf_op jit(solution)/shard_map/ppermute | solution.py:226
  61.4 19.4 %copy-start.2 = (bf16[1024,1024]{1,0:T(8,128)(2,1)S(1)}, bf16[1024,1024]{1,0:T(8,128)(2,1)}, u32[]{:S(2)}) copy-start(bf16[1024,1024]{1,0:T(8,128)(2,1)} %weight.1) | copy-start | bytes 6291460
  61.4 29.1 %collective-permute-start.6 = (bf16[256,1024]{1,0:T(8,128)(2,1)S(1)}, bf16[256,1024]{1,0:T(8,128)(2,1)S(1)}, u32[]{:S(2)}, u32[]{:S(2)}) collective-permute-start(bf16[256,1024]{1,0:T(8,128)(2,1)S(1)} %get-tuple-element.44), channel_id=1, source_target_pairs={{1,0},{2,1},{3,2},{0,3},{5,4},{6,5},{7,6},{4,7},{9,8},{10,9},{11,1... | collective-permute-start | bytes 1572872 | tf_op jit(solution)/shard_map/ppermute | solution.py:226
  62.6 31.0 %collective-permute-start.7 = (bf16[256,1024]{1,0:T(8,128)(2,1)S(1)}, bf16[256,1024]{1,0:T(8,128)(2,1)S(1)}, u32[]{:S(2)}, u32[]{:S(2)}) collective-permute-start(bf16[256,1024]{1,0:T(8,128)(2,1)S(1)} %get-tuple-element.45), channel_id=1, source_target_pairs={{3,0},{0,1},{1,2},{2,3},{7,4},{4,5},{5,6},{6,7},{11,8},{8,9},{9,10... | collective-permute-start | bytes 1572872 | tf_op jit(solution)/shard_map/ppermute | solution.py:226
  71.1 30.9 %collective-permute-start.8 = (bf16[256,1024]{1,0:T(8,128)(2,1)S(1)}, bf16[256,1024]{1,0:T(8,128)(2,1)S(1)}, u32[]{:S(2)}, u32[]{:S(2)}) collective-permute-start(bf16[256,1024]{1,0:T(8,128)(2,1)S(1)} %get-tuple-element.46), channel_id=1, source_target_pairs={{2,0},{3,1},{0,2},{1,3},{6,4},{7,5},{4,6},{5,7},{10,8},{11,9},{8,1... | collective-permute-start | bytes 1572872 | tf_op jit(solution)/shard_map/ppermute | solution.py:226
  79.3 9.9 %collective-permute-start.10 = (bf16[128,1024]{1,0:T(8,128)(2,1)S(1)}, bf16[128,1024]{1,0:T(8,128)(2,1)S(1)}, u32[]{:S(2)}, u32[]{:S(2)}) collective-permute-start(bf16[128,1024]{1,0:T(8,128)(2,1)S(1)} %collective-permute-done.3.far_a.refs_7_), channel_id=1, source_target_pairs={{0,4},{4,0},{1,5},{5,1},{2,6},{6,2},{3,7},{7,3},{8,12},{12,8},{9,1... | collective-permute-start | bytes 786440 | tf_op jit(solution)/shard_map/ppermute | solution.py:241
  80.7 9.7 %collective-permute-start.11 = (bf16[128,1024]{1,0:T(8,128)(2,1)S(1)}, bf16[128,1024]{1,0:T(8,128)(2,1)S(1)}, u32[]{:S(2)}, u32[]{:S(2)}) collective-permute-start(bf16[128,1024]{1,0:T(8,128)(2,1)S(1)} %collective-permute-done.4.far_b.refs_8_), channel_id=1, source_target_pairs={{0,4},{4,0},{1,5},{5,1},{2,6},{6,2},{3,7},{7,3},{8,12},{12,8},{9,1... | collective-permute-start | bytes 786440 | tf_op jit(solution)/shard_map/ppermute | solution.py:242
  89.2 19.5 %copy-start.4 = (bf16[2,256,1024]{2,1,0:T(8,128)(2,1)}, bf16[2,256,1024]{2,1,0:T(8,128)(2,1)S(1)}, u32[]{:S(2)}) copy-start(bf16[2,256,1024]{2,1,0:T(8,128)(2,1)S(1)} %get-tuple-element.63) | copy-start | bytes 3145732
  89.2 19.5 %copy-start.5 = (bf16[2,256,1024]{2,1,0:T(8,128)(2,1)}, bf16[2,256,1024]{2,1,0:T(8,128)(2,1)S(1)}, u32[]{:S(2)}) copy-start(bf16[2,256,1024]{2,1,0:T(8,128)(2,1)S(1)} %get-tuple-element.62) | copy-start | bytes 3145732
  108.7 7.1 %collective-permute-start.21 = (bf16[8,64,1024]{2,1,0:T(8,128)(2,1)S(1)}, bf16[8,64,1024]{2,1,0:T(8,128)(2,1)S(1)}, u32[]{:S(2)}, u32[]{:S(2)}) collective-permute-start(bf16[8,64,1024]{2,1,0:T(8,128)(2,1)S(1)} %get-tuple-element.72), channel_id=1, source_target_pairs={{0,8},{8,0},{1,9},{9,1},{2,10},{10,2},{3,11},{11,3},{4,12},{12,4},... | collective-permute-start | bytes 3145736 | tf_op jit(solution)/shard_map/ppermute | solution.py:265
  116.3 22.2 %copy-start.6 = (f32[1,64,1024]{2,1,0:T(8,128)S(1)}, f32[1,64,1024]{2,1,0:T(8,128)}, u32[]{:S(2)}) copy-start(f32[1,64,1024]{2,1,0:T(8,128)} %param.11) | copy-start | bytes 786436
  140.6 21.6 %all-to-all-start.1 = ((bf16[8,64,1024]{2,1,0:T(8,128)(2,1)}), bf16[8,64,1024]{2,1,0:T(8,128)(2,1)}, u32[]{:S(2)}, u32[]{:S(2)}) async-start(bf16[8,64,1024]{2,1,0:T(8,128)(2,1)} %broadcast_in_dim.36), calls=%async_computation.1 | async-start | bytes 2097152 | tf_op jit(solution)/shard_map/all_to_all | solution.py:272
  144.9 47.4 %collective-permute-start.18 = (bf16[2,256,1024]{2,1,0:T(8,128)(2,1)}, bf16[2,256,1024]{2,1,0:T(8,128)(2,1)S(1)}, u32[]{:S(2)}, u32[]{:S(2)}) collective-permute-start(bf16[2,256,1024]{2,1,0:T(8,128)(2,1)} %get-tuple-element.61), channel_id=1, source_target_pairs={{0,1},{1,2},{2,3},{3,0},{4,5},{5,6},{6,7},{7,4},{8,9},{9,10},{10,1... | collective-permute-start | bytes 3145736 | tf_op jit(solution)/shard_map/ppermute | solution.py:258
  145.0 47.4 %collective-permute-start.19 = (bf16[2,256,1024]{2,1,0:T(8,128)(2,1)}, bf16[2,256,1024]{2,1,0:T(8,128)(2,1)S(1)}, u32[]{:S(2)}, u32[]{:S(2)}) collective-permute-start(bf16[2,256,1024]{2,1,0:T(8,128)(2,1)} %copy-done.5), channel_id=1, source_target_pairs={{0,3},{1,0},{2,1},{3,2},{4,7},{5,4},{6,5},{7,6},{8,11},{9,8},{10,9... | collective-permute-start | bytes 3145736 | tf_op jit(solution)/shard_map/ppermute | solution.py:259
  147.6 44.7 %collective-permute-start.20 = (bf16[2,256,1024]{2,1,0:T(8,128)(2,1)}, bf16[2,256,1024]{2,1,0:T(8,128)(2,1)}, u32[]{:S(2)}, u32[]{:S(2)}) collective-permute-start(bf16[2,256,1024]{2,1,0:T(8,128)(2,1)} %copy-done.4), channel_id=1, source_target_pairs={{0,2},{1,3},{2,0},{3,1},{4,6},{5,7},{6,4},{7,5},{8,10},{9,11},{10,... | collective-permute-start | bytes 3145736 | tf_op jit(solution)/shard_map/ppermute | solution.py:260
  162.3 33.9 %collective-permute-start.22 = (bf16[8,64,1024]{2,1,0:T(8,128)(2,1)}, bf16[8,64,1024]{2,1,0:T(8,128)(2,1)}, u32[]{:S(2)}, u32[]{:S(2)}) collective-permute-start(bf16[8,64,1024]{2,1,0:T(8,128)(2,1)} %all-to-all-done.1), channel_id=1, source_target_pairs={{0,8},{8,0},{1,9},{9,1},{2,10},{10,2},{3,11},{11,3},{4,12},{12,4},... | collective-permute-start | bytes 3145736 | tf_op jit(solution)/shard_map/ppermute | solution.py:273
